TPU v7x, 256 devices: a whole 4x4x8 slice. The times are simulated.
256 devices in a mesh: replica: 16 (over z_hi, y), tensor: 16 (over x, z_lo, core).
Axes of the slice: x: 4, y: 4, z: 8 (z_hi: 4, z_lo: 2; z = z_hi * 2 + z_lo), core: 2. Of those that a mesh axis runs over, the one named last changes fastest.
Arguments:
- activations: bfloat16 [16384, 2048], P('replica', 'tensor'), may hold values from -0.625 to 0.625
- grad_out: bfloat16 [16384, 7168], P('replica', 'tensor'), may hold values from -6 to 6
- weight: bfloat16 [2048, 7168], P(None, 'tensor'), may hold values from -0.0625 to 0.0625
- momentum: float32 [16, 2048, 7168], P('replica', None, 'tensor'), may hold values from -6 to 6
- freq_rows: int32 [16, 32, 112], P(None, None, 'tensor'), may hold values from 0 to 63
Outputs:
- input_grad: bfloat16 [16384, 2048], P('replica', 'tensor')
- momentum_out: float32 [16, 2048, 7168], P('replica', None, 'tensor')
- update: bfloat16 [2048, 7168], P(None, 'tensor')
All inputs are finite; a program needn't handle non-finite values.
Results may differ from a plain program's by a relative error of at most 0.001.
Values may be sent and summed in bfloat16 or wider, within the bound.
A program may use at most 128 MiB of HBM per device.

v0:
```python
import jax
import jax.numpy as jnp
from jax import lax
from jax.sharding import PartitionSpec as P

TILE = 64


decay_rate = 0.9
highest = lax.Precision.HIGHEST


def cosine_table():
    freq = jnp.arange(TILE, dtype=jnp.float32)[:, None]
    place = jnp.arange(TILE, dtype=jnp.float32)[None, :]
    values = jnp.cos(jnp.pi * (2.0 * place + 1.0) * freq / (2.0 * TILE)) * jnp.sqrt(2.0 / TILE)
    return jnp.where(freq == 0.0, values / jnp.sqrt(2.0), values)


def decode(coeff_all, chosen_all, basis):
    onehot = (chosen_all[..., None] == jnp.arange(TILE, dtype=jnp.int32)).astype(jnp.float32)
    summed = jnp.einsum("rack,racj->ackj", onehot, coeff_all, precision=highest)
    right_done = jnp.einsum("ackj,jm->ackm", summed, basis, precision=highest)
    decoded = jnp.einsum("kn,ackm->ancm", basis, right_done, precision=highest)
    return decoded.reshape(summed.shape[0] * TILE, summed.shape[1] * TILE)


def body(activations, grad_out, weight, momentum, freq_rows):
    basis = cosine_table()
    partial_value = lax.dot_general(
        grad_out, weight, (((1,), (1,)), ((), ())), preferred_element_type=jnp.float32
    )
    input_grad = lax.psum_scatter(partial_value, "tensor", scatter_dimension=1, tiled=True).astype(
        jnp.bfloat16
    )
    weight_grad = lax.dot_general(
        lax.all_gather(activations, "tensor", axis=1, tiled=True),
        grad_out,
        (((0,), (0,)), ((), ())),
        preferred_element_type=jnp.float32,
    )
    feature_count = weight_grad.shape[0]
    hidden_count = weight_grad.shape[1]
    tile_rows = feature_count // TILE
    tile_cols = hidden_count // TILE
    kept = decay_rate * momentum[0] + weight_grad
    my_index = lax.axis_index("replica")
    chosen = lax.dynamic_index_in_dim(freq_rows, my_index, 0, keepdims=False)
    tile_view = kept.reshape(tile_rows, TILE, tile_cols, TILE)
    half_done = jnp.einsum("ancm,lm->ancl", tile_view, basis, precision=highest)
    onehot = (chosen[:, :, None] == jnp.arange(TILE, dtype=jnp.int32)[None, None, :]).astype(
        jnp.float32
    )
    picked = jnp.einsum("ack,kn->acn", onehot, basis, precision=highest)
    coeff_rows = jnp.einsum("acn,ancl->acl", picked, half_done, precision=highest)
    spread = jnp.einsum("acj,jm->acm", coeff_rows, basis, precision=highest)
    removed = jnp.einsum("acn,acm->ancm", picked, spread)
    momentum_out = (kept - removed.reshape(feature_count, hidden_count))[None]
    band = tile_rows // 4
    results = []
    for block_index in range(4):
        block_rows = coeff_rows[block_index * band : (block_index + 1) * band]
        gathered = lax.all_gather(block_rows[None], "replica", axis=0, tiled=True)
        block_chosen = freq_rows[:, block_index * band : (block_index + 1) * band]
        results.append(decode(gathered, block_chosen, basis))
    update = jnp.concatenate(results, axis=0).astype(jnp.bfloat16)
    return (input_grad, momentum_out, update)


def solution(mesh):
    placed = (
        P("replica", "tensor"),
        P("replica", "tensor"),
        P(None, "tensor"),
        P("replica", None, "tensor"),
        P(None, None, "tensor"),
    )
    return jax.shard_map(
        body,
        mesh=mesh,
        in_specs=placed,
        out_specs=(P("replica", "tensor"), P("replica", None, "tensor"), P(None, "tensor")),
        check_vma=False,
    )
```

profile of v0, /device:TPU:2, one launch (start us, length us, event | category | flops | bytes accessed | tf_op | source)
XLA Modules:
  0.0 345.1 jit_solution(10398331758102312585)
XLA Ops:
  7.2 0.0 copy-start
  7.2 0.0 all-gather.6.cloned.1.call-start
  7.2 0.7 all-gather.6.cloned.1.call-update
  7.9 0.0 reduce-scatter.2.cloned.1.call-start
  8.0 0.7 copy-done
  8.7 6.8 %fusion.128 = f32[1024,2048]{1,0:T(8,128)} fusion(bf16[1024,448]{0,1:T(8,128)(2,1)} %param.6, bf16[2048,448]{0,1:T(8,128)(2,1)S(1)} %copy-done), kind=kOutput, calls=%fused_computation.147 | convolution fusion | flops 1879048192 | bytes 11141120 | tf_op jit(solution)/shard_map/dot_general | solution.py:30
  15.5 0.0 copy-start.3
  15.5 0.0 reduce-scatter.2.cloned.1.call-update
  15.5 0.0 copy-start.6
  15.5 0.8 copy-done.3
  16.3 0.1 fusion.127
  16.4 0.2 copy.15
  16.6 0.2 copy.17
  16.7 0.2 copy.19
  16.9 0.2 copy.21
  17.1 0.3 fusion.20
  17.4 0.0 copy-start.4
  17.4 0.2 iota_compare_fusion.3
  17.7 0.2 iota_compare_fusion.2
  17.9 0.2 iota_compare_fusion.1
  18.1 0.2 iota_compare_fusion
  18.3 42.2 %all-gather.6.cloned.1.call-done = bf16[1024,2048]{1,0:T(8,128)(2,1)} async-done(((bf16[1024,128]{1,0:T(8,128)(2,1)}), bf16[1024,2048]{1,0:T(8,128)(2,1)}) %all-gather.6.cloned.1.call-update) | async-done | bytes 4194320 | tf_op jit(solution)/shard_map/all_gather | solution.py:37
  60.4 0.0 copy-done.6
  60.4 7.3 %bitcast_add_fusion = f32[2048,448]{0,1:T(8,128)} fusion(f32[1,2048,448]{1,2,0:T(8,128)} %param.8, bf16[1024,448]{0,1:T(8,128)(2,1)S(1)} %copy-done.6, bf16[1024,2048]{1,0:T(8,128)(2,1)} %all-gather.6.cloned.1.call-done), kind=kOutput, calls=%fused_computation.3 | convolution fusion | flops 1880883200 | bytes 12451840 | tf_op jit(solution)/shard_map/dot_general | solution.py:36
  67.7 7.9 %reshape.50 = f32[32,64,7,64]{1,0,3,2:T(8,128)} reshape(f32[2048,448]{0,1:T(8,128)} %bitcast_add_fusion) | data formatting | bytes 7340032 | tf_op jit(solution)/shard_map/reshape | solution.py:49
  75.6 16.1 %fusion = f32[32,64,7,64]{3,1,2,0:T(8,128)S(1)} fusion(f32[32,64,7,64]{1,0,3,2:T(8,128)} %reshape.50, f32[64]{0:T(128)S(1)} %add_multiply_fusion, pred[64]{0:T(512)(128)(4,1)S(1)} %iota_compare_fusion.6), kind=kOutput, calls=%fused_computation | convolution fusion | flops 704663552 | bytes 7340352 | tf_op jit(solution)/shard_map/ancm,lm->ancl/dot_general | solution.py:50
  91.7 0.0 copy-done.4
  91.7 6.2 %fusion.18 = f32[32,7,1,64]{3,2,1,0:T(1,128)S(1)} fusion(f32[32,64,7,64]{3,1,2,0:T(8,128)S(1)} %fusion, f32[32,7,64,1]{2,0,1,3:T(8,128)S(1)} %bitcast.92), kind=kOutput, calls=%fused_computation.31 | convolution fusion | flops 11010048 | bytes 3784704 | tf_op jit(solution)/shard_map/acn,ancl->acl/dot_general | solution.py:55
  98.0 51.0 %all-gather = f32[128,7,64]{2,0,1:T(8,128)S(1)} all-gather(f32[8,7,64]{2,0,1:T(8,128)S(1)} %get-tuple-element.3), channel_id=2, replica_groups=mesh['replica'=16,'tensor'=16] {'replica'}, dimensions={0}, use_global_device_ids=true | all-gather | bytes 243712 | tf_op jit(solution)/shard_map/all_gather | solution.py:63
  149.0 1.6 fusion.12
  150.6 5.4 %fusion.32 = f32[8,7,64,64]{2,3,1,0:T(8,128)S(1)} fusion(f32[8,7,64,64]{3,2,1,0:T(8,128)S(1)} %fusion.12, f32[64]{0:T(128)S(1)} %add_multiply_fusion, pred[64]{0:T(512)(128)(4,1)S(1)} %iota_compare_fusion.6), kind=kOutput, calls=%fused_computation.46 | convolution fusion | flops 176181248 | bytes 1835328 | tf_op jit(solution)/shard_map/ackj,jm->ackm/dot_general | solution.py:23
  156.0 1.7 fusion.2
  157.8 0.6 copy.16
  158.4 0.5 reshape.52
  158.9 42.6 %all-gather.1 = f32[128,7,64]{2,0,1:T(8,128)S(1)} all-gather(f32[8,7,64]{2,0,1:T(8,128)S(1)} %get-tuple-element.5), channel_id=3, replica_groups=mesh['replica'=16,'tensor'=16] {'replica'}, dimensions={0}, use_global_device_ids=true | all-gather | bytes 243712 | tf_op jit(solution)/shard_map/all_gather | solution.py:63
  201.5 1.6 fusion.10
  203.2 5.4 %fusion.29 = f32[8,7,64,64]{2,3,1,0:T(8,128)S(1)} fusion(f32[8,7,64,64]{3,2,1,0:T(8,128)S(1)} %fusion.10, f32[64]{0:T(128)S(1)} %add_multiply_fusion, pred[64]{0:T(512)(128)(4,1)S(1)} %iota_compare_fusion.6), kind=kOutput, calls=%fused_computation.43 | convolution fusion | flops 176181248 | bytes 1835328 | tf_op jit(solution)/shard_map/ackj,jm->ackm/dot_general | solution.py:23
  208.6 1.7 fusion.3
  210.3 0.6 copy.18
  210.9 0.5 reshape.53
  211.5 43.3 %all-gather.2 = f32[128,7,64]{2,0,1:T(8,128)S(1)} all-gather(f32[8,7,64]{2,0,1:T(8,128)S(1)} %get-tuple-element.4), channel_id=4, replica_groups=mesh['replica'=16,'tensor'=16] {'replica'}, dimensions={0}, use_global_device_ids=true | all-gather | bytes 243712 | tf_op jit(solution)/shard_map/all_gather | solution.py:63
  254.7 1.6 fusion.8
  256.4 5.4 %fusion.26 = f32[8,7,64,64]{2,3,1,0:T(8,128)S(1)} fusion(f32[8,7,64,64]{3,2,1,0:T(8,128)S(1)} %fusion.8, f32[64]{0:T(128)S(1)} %add_multiply_fusion, pred[64]{0:T(512)(128)(4,1)S(1)} %iota_compare_fusion.6), kind=kOutput, calls=%fused_computation.40 | convolution fusion | flops 176181248 | bytes 1835328 | tf_op jit(solution)/shard_map/ackj,jm->ackm/dot_general | solution.py:23
  261.8 1.7 fusion.4
  263.5 0.6 copy.20
  264.1 0.5 reshape.54
  264.7 41.5 %all-gather.3 = f32[128,7,64]{2,0,1:T(8,128)S(1)} all-gather(f32[8,7,64]{2,0,1:T(8,128)S(1)} %get-tuple-element.6), channel_id=5, replica_groups=mesh['replica'=16,'tensor'=16] {'replica'}, dimensions={0}, use_global_device_ids=true | all-gather | bytes 243712 | tf_op jit(solution)/shard_map/all_gather | solution.py:63
  306.2 1.6 fusion.6
  307.8 5.4 %fusion.23 = f32[8,7,64,64]{2,3,1,0:T(8,128)S(1)} fusion(f32[8,7,64,64]{3,2,1,0:T(8,128)S(1)} %fusion.6, f32[64]{0:T(128)S(1)} %add_multiply_fusion, pred[64]{0:T(512)(128)(4,1)S(1)} %iota_compare_fusion.6), kind=kOutput, calls=%fused_computation.37 | convolution fusion | flops 176181248 | bytes 1835328 | tf_op jit(solution)/shard_map/ackj,jm->ackm/dot_general | solution.py:23
  313.3 1.7 fusion.5
  315.0 0.0 copy-start.5
  315.0 0.6 copy.22
  315.6 0.5 reshape.55
  316.2 0.8 fusion.35
  317.0 0.0 copy-done.5
  317.0 4.3 %multiply_bitcast_fusion = f32[32,64,7,64]{1,0,3,2:T(8,128)} fusion(f32[32,7,64]{2,0,1:T(8,128)S(1)} %copy-done.5, f32[32,7,64]{0,2,1:T(8,128)S(1)} %fusion.35), kind=kLoop, calls=%fused_computation.2 | loop fusion | flops 917504 | bytes 3784704 | tf_op jit(solution)/shard_map/acn,acm->ancm/transpose | solution.py:57
  321.3 7.5 %reshape.51 = f32[2048,448]{0,1:T(8,128)} reshape(f32[32,64,7,64]{1,0,3,2:T(8,128)} %multiply_bitcast_fusion) | data formatting | bytes 7340032 | tf_op jit(solution)/shard_map/reshape | solution.py:58
  328.8 0.0 copy-start.2
  328.8 1.5 pad_maximum_fusion
  330.3 1.2 copy-done.2
  331.5 0.0 copy-start.1
  331.5 4.8 %subtract_bitcast_fusion = f32[1,2048,448]{1,2,0:T(8,128)} fusion(f32[2048,448]{0,1:T(8,128)S(1)} %copy-done.2, f32[2048,448]{0,1:T(8,128)} %reshape.51), kind=kLoop, calls=%fused_computation.4 | loop fusion | flops 917504 | bytes 11010048 | tf_op jit(solution)/shard_map/broadcast_in_dim | solution.py:58
  336.3 1.8 convert_element_type.2
  338.0 0.0 copy-done.1
  (7 shorter events, 0.1 us)
Async XLA Ops:
  7.2 1.5 copy-start
  7.2 53.3 %all-gather.6.cloned.1.call-start = ((), (), s32[]{:S(2)}) async-start(), calls=%async_computation.2 | async-start | bytes 4456448 | tf_op jit(solution)/shard_map/all_gather | solution.py:37
  7.9 328.4 %reduce-scatter.2.cloned.1.call-start = ((), (), s32[]{:S(2)}) async-start(), calls=%async_computation.1 | async-start | bytes 8912896 | tf_op jit(solution)/shard_map/reduce_scatter | solution.py:33
  15.5 0.8 copy-start.3
  15.5 45.0 %copy-start.6 = (bf16[1024,448]{0,1:T(8,128)(2,1)S(1)}, bf16[1024,448]{0,1:T(8,128)(2,1)}, u32[]{:S(2)}) copy-start(bf16[1024,448]{0,1:T(8,128)(2,1)} %param.6) | copy-start | bytes 2752516
  17.4 74.3 %copy-start.4 = (f32[32,7,64]{2,0,1:T(8,128)}, f32[32,7,64]{2,0,1:T(8,128)S(1)}, u32[]{:S(2)}) copy-start(f32[32,7,64]{2,0,1:T(8,128)S(1)} %fusion.20) | copy-start | bytes 172036
  315.0 2.0 copy-start.5
  328.8 2.7 copy-start.2
  331.5 6.5 %copy-start.1 = (bf16[2048,448]{0,1:T(8,128)(2,1)S(1)}, bf16[2048,448]{0,1:T(8,128)(2,1)}, u32[]{:S(2)}) copy-start(bf16[2048,448]{0,1:T(8,128)(2,1)} %param.7) | copy-start | bytes 5505028
Sparse Core Ops, SparseCore 0:
  9.8 50.6 all-gather.5
  63.0 111.4 reduce-scatter.1
where the time goes:
time: 351 us; the launch traced here: 345 us
  blocking collectives  178 us (51%)
  matrix products  72.6 us (21%)
  waiting for transfers between devices  42.9 us (12%)
  local copies, waits for them, and re-layouts  23.5 us (7%)
  between operations  14.5 us (4%)
  other arithmetic  13.2 us (4%)
    all_gather x4, blocking collectives, body(): gathered = lax.all_gather(block_rows[None], 'replica', axis=0, tiled=True)  178 us
    all_gather x1, waiting for transfers between devices, body(): lax.all_gather(activations, 'tensor', axis=1, tiled=True)  42.2 us
    dot_general x4, matrix products, decode(): right_done = jnp.einsum('ackj,jm->ackm', summed, basis, precision=highest)  21.8 us
    dot_general x1, matrix products, body(): half_done = jnp.einsum('ancm,lm->ancl', tile_view, basis, precision=highest)  16.1 us
    reshape x1, local copies, waits for them, and re-layouts, body(): tile_view = kept.reshape(tile_rows, TILE, tile_cols, TILE)  7.87 us
    reshape x1, local copies, waits for them, and re-layouts, body(): momentum_out = (kept - removed.reshape(feature_count, hidden_count))[None]  7.48 us
    dot_general x1, matrix products, body(): lax.dot_general(lax.all_gather(activations, 'tensor', axis=1, tiled=True)...  7.29 us
  transfers between devices with their start and end apart: 2, of which 1 were waited for; matrix products, arithmetic and copies ran while one was open for 30% of the time, Pallas kernels for 0%

commit v1 on v0

v1 whole, which is shorter than its diff:
```python
import functools

import jax
import jax.numpy as jnp
import numpy as np
from jax import lax
from jax.experimental import pallas as pl
from jax.experimental.pallas import tpu as pltpu
from jax.sharding import PartitionSpec as P

MESH = pl.DeviceIdType.MESH
F32 = jnp.float32
BF16 = jnp.bfloat16

TILE = 64
decay_rate = 0.9


def cosine_pieces():
    freq = np.arange(TILE, dtype=np.float64)[:, None]
    place = np.arange(TILE, dtype=np.float64)[None, :]
    values = np.cos(np.pi * (2.0 * place + 1.0) * freq / (2.0 * TILE)) * np.sqrt(2.0 / TILE)
    values = np.where(freq == 0.0, values / np.sqrt(2.0), values).T
    rest = values.astype(np.float32)
    terms = []
    for _ in range(3):
        term = rest.astype(BF16)
        terms.append(term)
        rest = rest - term.astype(np.float32)
    terms.append(np.zeros_like(terms[0]))
    return np.concatenate(terms, axis=1)


def kernel(
    act_hbm, go_hbm, w_hbm, mom_hbm, freq_ref, cos_ref,
    ig_hbm, mo_hbm, up_hbm,
    act_raw, acts, go, wt, q, rx, zr, mom, gtmp, basis, left_side, p_own, p_all, upd, ig, fexp, vexp,
    load_sem, store_sem, ex_send, ex_recv, ag_send, ag_recv, sib_send, sib_recv,
    rs_send, rs_recv, zs_send, zs_recv, ps_send, ps_recv, py_send, py_recv,
):
    r = lax.axis_index("replica")
    t = lax.axis_index("tensor")
    x, z, c = t // 4, (t // 2) % 2, t % 2
    zh, y = r // 4, r % 4
    other = 1 - z

    def at(x_, z_, c_):
        return (r, x_ * 4 + z_ * 2 + c_)

    xr, xl, xo = (x + 1) % 4, (x + 3) % 4, (x + 2) % 4
    right, left = at(xr, z, c), at(xl, z, c)
    zdev, sib = at(x, other, c), at(x, z, 1 - c)
    zh_devs = [(((zh + k) % 4) * 4 + y, t) for k in (1, 2, 3)]
    y_devs = [(zh * 4 + (y + k) % 4, t) for k in (1, 2, 3)]

    loads = [
        pltpu.make_async_copy(act_hbm, act_raw, load_sem.at[0]),
        pltpu.make_async_copy(go_hbm, go.at[0], load_sem.at[1]),
        pltpu.make_async_copy(w_hbm.at[:, c], wt.at[0], load_sem.at[2]),
        pltpu.make_async_copy(mom_hbm, mom, load_sem.at[3]),
    ]
    for load in loads:
        load.start()

    barrier = pltpu.get_barrier_semaphore()
    peers = [right, left, zdev, sib] + zh_devs + y_devs
    for peer in peers:
        pl.semaphore_signal(barrier, inc=1, device_id=peer, device_id_type=MESH)

    loads[0].wait()
    acts[t] = jnp.transpose(act_raw[...])
    pl.semaphore_wait(barrier, len(peers))

    def remote(src, dst, send, recv, dev):
        return pltpu.make_async_remote_copy(
            src_ref=src, dst_ref=dst, send_sem=send, recv_sem=recv, device_id=dev, device_id_type=MESH
        )

    sent = []

    def push(src, dst, send, recv, dev):
        copy = remote(src, dst, send, recv, dev)
        copy.start()
        sent.append(copy)

    def block(x_, z_, c_):
        return acts.at[x_ * 4 + z_ * 2 + c_]

    def half(x_, z_, c_, k):
        return acts.at[x_ * 4 + z_ * 2 + c_, pl.ds(k * 64, 64)]

    def push_same(ref, sends, recvs, k, dev):
        push(ref, ref, sends.at[k], recvs.at[k], dev)

    def arrived(ref, sends, recvs, k):
        remote(ref, ref, sends.at[k], recvs.at[k], sib).wait_recv()

    own = block(x, z, c)
    push_same(own, ag_send, ag_recv, 0, right)
    push_same(own, ag_send, ag_recv, 1, left)
    push_same(own, ag_send, ag_recv, 4, zdev)
    push(go_hbm, go.at[1], ex_send.at[0], ex_recv.at[0], sib)
    push(w_hbm.at[:, 1 - c], wt.at[1], ex_send.at[1], ex_recv.at[1], sib)
    push_same(own, sib_send, sib_recv, 0, sib)

    lane_tile = lax.broadcasted_iota(jnp.int32, (32, 448), 1) // TILE
    mine = freq_ref[r]
    spread = jnp.zeros((32, 448), jnp.int32)
    for k in range(7):
        spread = jnp.where(lane_tile == k, mine[:, k : k + 1], spread)
    fexp[...] = spread
    lane = lax.broadcasted_iota(jnp.int32, (32, 128), 1)
    folded = jnp.full((32, 128), -1, jnp.int32)
    for rep in range(16):
        rows = freq_ref[rep]
        for k in range(7):
            folded = jnp.where(lane == k * 16 + rep, rows[:, k : k + 1], folded)
    vexp[...] = folded

    def onehot4(row, width):
        hot = (lax.broadcasted_iota(jnp.int32, (TILE, width), 0) == row).astype(F32).astype(BF16)
        return jnp.concatenate([hot] * 4, axis=0)

    @pl.loop(0, 32)
    def _(a):
        rows = pl.ds(pl.multiple_of(a * TILE, TILE), TILE)
        basis[rows, :] = jnp.dot(cos_ref[...], onehot4(fexp[pl.ds(a, 1), :], 448), preferred_element_type=F32)
        side = jnp.dot(cos_ref[...], onehot4(vexp[pl.ds(a, 1), :], 128), preferred_element_type=F32)
        high = side.astype(BF16)
        low = (side - high.astype(F32)).astype(BF16)
        left_side[rows, :] = jnp.concatenate([high, high, low], axis=1)

    loads[1].wait()
    loads[2].wait()
    remote(go.at[0], go.at[1], ex_send.at[0], ex_recv.at[0], sib).wait_recv()
    remote(wt.at[0], wt.at[1], ex_send.at[1], ex_recv.at[1], sib).wait_recv()

    def share(dx):
        dest = (x + dx) % 4

        @pl.loop(0, 4)
        def _(k):
            rows = pl.ds(pl.multiple_of(k * 256, 256), 256)
            total = jnp.zeros((256, 256), F32)
            for part in range(2):
                wpair = wt[part, pl.ds(dest * 2, 2)].reshape(256, 448)
                total += lax.dot_general(
                    go[part, rows, :], wpair, (((1,), (1,)), ((), ())), preferred_element_type=F32
                )
            q[dx, 0, rows, :] = total[:, :128]
            q[dx, 1, rows, :] = total[:, 128:]

    top, bottom = pl.ds(0, 512), pl.ds(512, 512)
    zs = (other, z)

    def rs_push(src, direction, kind, zi):
        k = (direction * 3 + kind) * 2 + zi
        push(src, rx.at[direction, kind, zi], rs_send.at[k], rs_recv.at[k], (right, left)[direction])

    def rs_wait(direction, kind, zi):
        k = (direction * 3 + kind) * 2 + zi
        slot = rx.at[direction, kind, zi]
        remote(slot, slot, rs_send.at[k], rs_recv.at[k], sib).wait_recv()

    share(2)
    rs_push(q.at[2, zs[0], top], 0, 0, 0)
    rs_push(q.at[2, zs[0], bottom], 1, 0, 0)
    share(1)
    rs_push(q.at[1, zs[0], bottom], 0, 1, 0)
    share(3)
    rs_push(q.at[3, zs[0], top], 1, 1, 0)
    share(0)

    def from_x(x_, k, fwd_half, fwd_k, fwd_dev, zk):
        blk = block(x_, z, c)
        arrived(blk, ag_send, ag_recv, k)
        push_same(half(x_, z, c, fwd_half), ag_send, ag_recv, fwd_k, fwd_dev)
        push_same(blk, ag_send, ag_recv, zk, zdev)
        push_same(blk, sib_send, sib_recv, zk - 4, sib)

    from_x(xl, 0, 0, 2, right, 5)
    from_x(xr, 1, 1, 3, left, 6)
    rs_push(q.at[2, zs[1], top], 0, 0, 1)
    rs_push(q.at[2, zs[1], bottom], 1, 0, 1)
    rs_push(q.at[1, zs[1], bottom], 0, 1, 1)
    rs_push(q.at[3, zs[1], top], 1, 1, 1)

    loads[3].wait()

    def unit(x_, z_):
        u = x_ * 2 + z_
        pair = acts[pl.ds(u * 2, 2)].reshape(256, 1024)
        gtmp[...] = jnp.dot(pair, go[0], preferred_element_type=F32)
        base = u * 256

        @pl.loop(0, 4)
        def _(s):
            rows = pl.ds(pl.multiple_of(base + s * TILE, TILE), TILE)
            kept = decay_rate * mom[rows, :] + gtmp[pl.ds(pl.multiple_of(s * TILE, TILE), TILE), :]
            mine = basis[rows, :]
            line = jnp.sum(mine * kept, axis=0, keepdims=True)
            mom[rows, :] = kept - mine * line
            p_own[z_, pl.ds(x_ * 4 + s, 1), :] = line

        rows = pl.ds(pl.multiple_of(base, 256), 256)
        copy = pltpu.make_async_copy(mom.at[rows], mo_hbm.at[rows], store_sem.at[len(stores)])
        copy.start()
        stores.append(copy)

    stores = []
    sb = lambda x_, z_: block(x_, z_, 1 - c)
    sh = lambda x_, z_, k: half(x_, z_, 1 - c, k)

    arrived(sb(x, z), sib_send, sib_recv, 0)
    unit(x, z)
    arrived(sb(xl, z), sib_send, sib_recv, 1)
    unit(xl, z)
    arrived(sb(xr, z), sib_send, sib_recv, 2)
    unit(xr, z)
    for k in range(2):
        piece = half(xo, z, c, k)
        arrived(piece, ag_send, ag_recv, 2 + k)
        push_same(piece, ag_send, ag_recv, 7 + k, zdev)
        push_same(piece, sib_send, sib_recv, 3 + k, sib)
    for k in range(2):
        arrived(sh(xo, z, k), sib_send, sib_recv, 3 + k)
    unit(xo, z)

    def p_zh(group, z_):
        rows = pl.ds(pl.multiple_of(z_ * 16, 16), 16)
        p_all[zh, y, rows, :] = p_own[z_]
        mine = p_all.at[zh, y, rows]
        for k, dev in enumerate(zh_devs):
            push(mine, mine, ps_send.at[group, k], ps_recv.at[group, k], dev)

    def p_y(group, z_):
        rows = pl.ds(pl.multiple_of(z_ * 16, 16), 16)
        for k in range(3):
            slot = p_all.at[(zh + 3 - k) % 4, y, rows]
            remote(slot, slot, ps_send.at[group, k], ps_recv.at[group, k], sib).wait_recv()
        mine = p_all.at[:, y, rows]
        for k, dev in enumerate(y_devs):
            push(mine, mine, py_send.at[group, k], py_recv.at[group, k], dev)

    def p_done(group, z_):
        rows = pl.ds(pl.multiple_of(z_ * 16, 16), 16)
        for k in range(3):
            slot = p_all.at[:, (y + 3 - k) % 4, rows]
            remote(slot, slot, py_send.at[group, k], py_recv.at[group, k], sib).wait_recv()

    tiles = lax.broadcasted_iota(jnp.int32, (16, 448), 1) // TILE

    def decode(z_):
        @pl.loop(0, 16)
        def _(i):
            a = (i // 4) * 8 + z_ * 4 + i % 4
            row = pl.ds(z_ * 16 + i, 1)
            p16 = jnp.concatenate([p_all[k // 4, k % 4, row, :] for k in range(16)], axis=0)
            high = p16.astype(BF16).astype(F32)
            low = p16 - high
            zero = jnp.zeros_like(p16)
            highs = [jnp.where(tiles == k, high, zero).astype(BF16) for k in range(7)] + [zero.astype(BF16)]
            lows = [jnp.where(tiles == k, low, zero).astype(BF16) for k in range(7)] + [zero.astype(BF16)]
            full = jnp.concatenate(highs + lows + highs, axis=0)
            rows = pl.ds(pl.multiple_of(a * TILE, TILE), TILE)
            upd[rows, :] = jnp.dot(left_side[rows, :], full, preferred_element_type=F32).astype(BF16)

        for k in range(4):
            rows = pl.ds(pl.multiple_of((k * 2 + z_) * 256, 256), 256)
            copy = pltpu.make_async_copy(upd.at[rows], up_hbm.at[rows], store_sem.at[len(stores)])
            copy.start()
            stores.append(copy)

    p_zh(0, z)

    def rs_second(zi):
        rs_wait(0, 0, zi)
        q[1, zs[zi], top, :] += rx[0, 0, zi]
        rs_push(q.at[1, zs[zi], top], 0, 2, zi)
        rs_wait(1, 0, zi)
        q[3, zs[zi], bottom, :] += rx[1, 0, zi]
        rs_push(q.at[3, zs[zi], bottom], 1, 2, zi)

    rs_second(0)
    p_y(0, z)

    def from_z(x_, zk):
        blk = block(x_, other, c)
        arrived(blk, ag_send, ag_recv, zk)
        push_same(blk, sib_send, sib_recv, zk + 1, sib)

    from_z(x, 4)
    from_z(xl, 5)
    from_z(xr, 6)
    arrived(sb(x, other), sib_send, sib_recv, 5)
    unit(x, other)
    arrived(sb(xl, other), sib_send, sib_recv, 6)
    unit(xl, other)
    arrived(sb(xr, other), sib_send, sib_recv, 7)
    unit(xr, other)
    rs_second(1)
    for k in range(2):
        piece = half(xo, other, c, k)
        arrived(piece, ag_send, ag_recv, 7 + k)
        push_same(piece, sib_send, sib_recv, 8 + k, sib)
    for k in range(2):
        arrived(sh(xo, other, k), sib_send, sib_recv, 8 + k)
    unit(xo, other)
    p_zh(1, other)

    def x_sum(zi):
        for direction in range(2):
            for kind in (1, 2):
                rs_wait(direction, kind, zi)
        q[0, zs[zi], top, :] += rx[0, 2, zi] + rx[1, 1, zi]
        q[0, zs[zi], bottom, :] += rx[0, 1, zi] + rx[1, 2, zi]

    x_sum(0)
    push(q.at[0, other], zr, zs_send, zs_recv, zdev)
    p_done(0, z)
    decode(z)
    p_y(1, other)
    p_done(1, other)
    decode(other)

    x_sum(1)
    remote(q.at[0, other], zr, zs_send, zs_recv, zdev).wait_recv()
    ig[...] = (q[0, z] + zr[...]).astype(BF16)
    last = pltpu.make_async_copy(ig, ig_hbm, store_sem.at[len(stores)])
    last.start()
    for copy in stores:
        copy.wait()
    last.wait()
    for copy in sent:
        copy.wait_send()


def body(activations, grad_out, weight, momentum, freq_rows):
    hbm = pl.BlockSpec(memory_space=pl.ANY)
    vmem = pl.BlockSpec(memory_space=pltpu.VMEM)
    dma = pltpu.SemaphoreType.DMA
    input_grad, momentum_out, update = pl.pallas_call(
        kernel,
        out_shape=(
            jax.ShapeDtypeStruct((1024, 128), BF16),
            jax.ShapeDtypeStruct((2048, 448), F32),
            jax.ShapeDtypeStruct((2048, 448), BF16),
        ),
        in_specs=[hbm, hbm, hbm, hbm, vmem, vmem],
        out_specs=(hbm, hbm, hbm),
        scratch_shapes=[
            pltpu.VMEM((1024, 128), BF16),
            pltpu.VMEM((16, 128, 1024), BF16),
            pltpu.VMEM((2, 1024, 448), BF16),
            pltpu.VMEM((2, 8, 128, 448), BF16),
            pltpu.VMEM((4, 2, 1024, 128), F32),
            pltpu.VMEM((2, 3, 2, 512, 128), F32),
            pltpu.VMEM((1024, 128), F32),
            pltpu.VMEM((2048, 448), F32),
            pltpu.VMEM((256, 448), F32),
            pltpu.VMEM((2048, 448), F32),
            pltpu.VMEM((2048, 384), BF16),
            pltpu.VMEM((2, 16, 448), F32),
            pltpu.VMEM((4, 4, 32, 448), F32),
            pltpu.VMEM((2048, 448), BF16),
            pltpu.VMEM((1024, 128), BF16),
            pltpu.VMEM((32, 448), jnp.int32),
            pltpu.VMEM((32, 128), jnp.int32),
            dma((4,)), dma((17,)),
            dma((2,)), dma((2,)),
            dma((9,)), dma((9,)),
            dma((10,)), dma((10,)),
            dma((12,)), dma((12,)),
            dma, dma,
            dma((2, 3)), dma((2, 3)),
            dma((2, 3)), dma((2, 3)),
        ],
        compiler_params=pltpu.CompilerParams(
            collective_id=0, has_side_effects=True, vmem_limit_bytes=52 * 1024 * 1024
        ),
        name="demo_step",
    )(
        activations,
        grad_out,
        weight.reshape(8, 2, 128, 448),
        momentum[0],
        freq_rows,
        jnp.asarray(cosine_pieces()),
    )
    return input_grad, momentum_out[None], update


def solution(mesh):
    placed = (
        P("replica", "tensor"),
        P("replica", "tensor"),
        P(None, "tensor"),
        P("replica", None, "tensor"),
        P(None, None, "tensor"),
    )
    return jax.shard_map(
        body,
        mesh=mesh,
        in_specs=placed,
        out_specs=(P("replica", "tensor"), P("replica", None, "tensor"), P(None, "tensor")),
        check_vma=False,
    )
```

time: 351 us -> 87.9 us (0.25); the launches traced: 345 us -> 87.4 us
  blocking collectives: 178 us -> 0 us
  matrix products: 72.6 us -> 0 us
  Pallas kernels: 0 us -> 66.8 us
  waiting for transfers between devices: 42.9 us -> 0 us
  between operations: 14.5 us -> 0.66 us
  other arithmetic: 13.2 us -> 0 us
  local copies, waits for them, and re-layouts: 23.5 us -> 19.9 us
    all_gather x4 -> x0, blocking collectives: 178 us -> none  [body(): gathered = lax.all_gather(block_rows[None], 'replica', axis=0, tiled=True)]
    dot_general x18 -> x0, matrix products: 72.6 us -> none  [the longest x4 21.8 us: decode(): right_done = jnp.einsum('ackj,jm->ackm', summed, basis, precision=highest)]
    pallas_call x0 -> x1, Pallas kernels: none -> 66.8 us  [body(): pl.pallas_call(kernel, out_shape=(jax.ShapeDtypeStruct((1024, 128), BF16)...]
    all_gather x1 -> x0, waiting for transfers between devices: 42.2 us -> none  [body(): lax.all_gather(activations, 'tensor', axis=1, tiled=True)]
    reshape x6 -> x0, local copies, waits for them, and re-layouts: 17.5 us -> none  [the longest x1 7.87 us: body(): tile_view = kept.reshape(tile_rows, TILE, tile_cols, TILE)]
    unnamed x15 -> x13, local copies, waits for them, and re-layouts: 2.73 us -> 19.9 us
    broadcast_in_dim x1 -> x0, other arithmetic: 4.76 us -> none  [body(): momentum_out = (kept - removed.reshape(feature_count, hidden_count))[None]]
    transpose x1 -> x0, other arithmetic: 4.34 us -> none  [body(): removed = jnp.einsum('acn,acm->ancm', picked, spread)]
  transfers between devices with their start and end apart: 2 -> 0, of which waited for: 1 -> 0; matrix products, arithmetic and copies ran while one was open for 30% -> 0% of each run, Pallas kernels for 0% -> 0%
where the time goes in v1:
time: 87.9 us; the launch traced here: 87.4 us
  Pallas kernels  66.8 us (76%)
  local copies, waits for them, and re-layouts  19.9 us (23%)
    pallas_call x1, Pallas kernels, body(): pl.pallas_call(kernel, out_shape=(jax.ShapeDtypeStruct((1024, 128), BF16)...  66.8 us
    unnamed x13, local copies, waits for them, and re-layouts  19.9 us

profile of v1, /device:TPU:2, one launch (start us, length us, event | category | flops | bytes accessed | tf_op | source)
XLA Modules:
  0.0 87.4 jit_solution(927176408714950806)
XLA Ops:
  0.6 1.0 %copy.12.freq_ref = s32[16,32,7]{2,1,0:T(8,128)S(1)} copy(s32[16,32,7]{1,0,2:T(8,128)} %param.10) | data formatting | bytes 28672 | tf_op args[4]
  1.6 1.5 %copy.11.go_hbm = bf16[1024,448]{1,0:T(8,128)(2,1)S(1)} copy(bf16[1024,448]{0,1:T(8,128)(2,1)} %param.7) | data formatting | bytes 1835008 | tf_op args[1]
  3.1 3.8 %copy.9 = bf16[2048,448]{1,0:T(8,128)(2,1)} copy(bf16[2048,448]{0,1:T(8,128)(2,1)} %param.8) | data formatting | bytes 3670016 | tf_op args[2]
  6.9 0.0 copy-start
  6.9 0.0 copy-start.1
  6.9 5.2 %copy.10 = f32[1,2048,448]{2,1,0:T(8,128)} copy(f32[1,2048,448]{1,2,0:T(8,128)} %param.9) | data formatting | bytes 7340032 | tf_op args[3]
  12.1 0.0 copy-done
  12.1 0.0 copy-done.1
  12.1 66.8 %demo_step.1 = (bf16[1024,128]{1,0:T(8,128)(2,1)S(1)}, f32[2048,448]{1,0:T(8,128)}, bf16[2048,448]{1,0:T(8,128)(2,1)}) custom-call(bf16[1024,128]{1,0:T(8,128)(2,1)S(1)} %copy-done, bf16[1024,448]{1,0:T(8,128)(2,1)S(1)} %copy.11.go_hbm, bf16[8,2,128,448]{3,2,1,0:T(8,128)(2,1)} %bitcast.4, f32[2048,448]{1,0:T(8,128)} %bitcast.3, ...), custom_call_target="tpu_custom_call" | custom-call | tf_op jit(solution)/shard_map/demo_step/pallas_call | solution.py:342
  79.0 0.0 copy-start.2
  79.0 5.4 %copy.13 = f32[1,2048,448]{1,2,0:T(8,128)} copy(f32[1,2048,448]{2,1,0:T(8,128)} %bitcast.5) | data formatting | bytes 7340032
  84.4 0.0 copy-done.2
  84.4 2.3 %copy.14 = bf16[2048,448]{0,1:T(8,128)(2,1)} copy(bf16[2048,448]{1,0:T(8,128)(2,1)S(1)} %copy-done.2) | data formatting | bytes 3670016
  86.6 0.7 copy.16
Async XLA Ops:
  6.9 5.2 %copy-start = (bf16[1024,128]{1,0:T(8,128)(2,1)S(1)}, bf16[1024,128]{1,0:T(8,128)(2,1)}, u32[]{:S(2)}) copy-start(bf16[1024,128]{1,0:T(8,128)(2,1)} %act_hbm.1) | copy-start | bytes 786436
  6.9 5.2 %copy-start.1 = (bf16[64,256]{1,0:T(8,128)(2,1)S(1)}, bf16[64,256]{1,0:T(8,128)(2,1)}, u32[]{:S(2)}) copy-start(bf16[64,256]{1,0:T(8,128)(2,1)} %constant.2.clone.cos_ref) | copy-start | bytes 98308
  79.0 5.4 %copy-start.2 = (bf16[2048,448]{1,0:T(8,128)(2,1)S(1)}, bf16[2048,448]{1,0:T(8,128)(2,1)}, u32[]{:S(2)}) copy-start(bf16[2048,448]{1,0:T(8,128)(2,1)} %get-tuple-element.11) | copy-start | bytes 5505028

commit v2 on v1

v2 whole, which is shorter than its diff:
```python
import functools

import jax
import jax.numpy as jnp
import numpy as np
from jax import lax
from jax.experimental import pallas as pl
from jax.experimental.pallas import tpu as pltpu
from jax.sharding import PartitionSpec as P

MESH = pl.DeviceIdType.MESH
F32 = jnp.float32
BF16 = jnp.bfloat16

TILE = 64
decay_rate = 0.9


def cosine_tables():
    freq = np.arange(TILE, dtype=np.float64)[:, None]
    place = np.arange(TILE, dtype=np.float64)[None, :]
    values = np.cos(np.pi * (2.0 * place + 1.0) * freq / (2.0 * TILE)) * np.sqrt(2.0 / TILE)
    values = np.where(freq == 0.0, values / np.sqrt(2.0), values).astype(np.float32)
    high = values.astype(BF16)
    low = (values - high.astype(np.float32)).astype(BF16)
    return np.concatenate([values] * 2, axis=1), np.concatenate([high] * 4 + [low] * 4, axis=1)


def kernel(
    act_hbm, go_hbm, w_hbm, mom_hbm, freq_hbm, cos_hbm, terms_hbm,
    ig_hbm, mo_hbm, up_hbm,
    acts, got, go, wt, q, sx, rx, sz, rz, mom, gtmp, ptmp, ycat, basis, segments, right_side, lhs, p_own, p_all, upd, ig,
    freq_ref, cos_ref, terms_ref,
    load_sem, store_sem, ex_send, ex_recv, ag_send, ag_recv, sib_send, sib_recv,
    rs_send, rs_recv, zs_send, zs_recv, ps_send, ps_recv, py_send, py_recv,
):
    r = lax.axis_index("replica")
    t = lax.axis_index("tensor")
    x, z, c = t // 4, (t // 2) % 2, t % 2
    zh, y = r // 4, r % 4
    other = 1 - z

    def at(x_, z_, c_):
        return (r, x_ * 4 + z_ * 2 + c_)

    xr, xl, xo = (x + 1) % 4, (x + 3) % 4, (x + 2) % 4
    right, left = at(xr, z, c), at(xl, z, c)
    zdev, sib = at(x, other, c), at(x, z, 1 - c)
    zh_devs = [(((zh + k) % 4) * 4 + y, t) for k in (1, 2, 3)]
    y_devs = [(zh * 4 + (y + k) % 4, t) for k in (1, 2, 3)]

    def w_cols(u, c_):
        return w_hbm.at[:, pl.ds(pl.multiple_of((2 * u + c_) * 128, 128), 128)]

    loads = [
        pltpu.make_async_copy(go_hbm, got, load_sem.at[0]),
        pltpu.make_async_copy(act_hbm, acts.at[t], load_sem.at[1]),
        pltpu.make_async_copy(freq_hbm, freq_ref, load_sem.at[2]),
        pltpu.make_async_copy(cos_hbm, cos_ref, load_sem.at[3]),
        pltpu.make_async_copy(terms_hbm, terms_ref, load_sem.at[4]),
    ] + [pltpu.make_async_copy(w_cols(u, c), wt.at[0, u], load_sem.at[5 + u]) for u in range(8)]
    loads.append(pltpu.make_async_copy(mom_hbm, mom, load_sem.at[13]))
    for load in loads:
        load.start()

    barrier = pltpu.get_barrier_semaphore()
    peers = [right, left, zdev, sib] + zh_devs + y_devs
    for peer in peers:
        pl.semaphore_signal(barrier, inc=1, device_id=peer, device_id_type=MESH)

    loads[0].wait()
    go[0] = jnp.transpose(got[...])
    loads[1].wait()
    pl.semaphore_wait(barrier, len(peers))

    def remote(src, dst, send, recv, dev):
        return pltpu.make_async_remote_copy(
            src_ref=src, dst_ref=dst, send_sem=send, recv_sem=recv, device_id=dev, device_id_type=MESH
        )

    sent = []

    def push(src, dst, send, recv, dev):
        copy = remote(src, dst, send, recv, dev)
        copy.start()
        sent.append(copy)

    def block(x_, z_, c_):
        return acts.at[x_ * 4 + z_ * 2 + c_]

    def half(x_, z_, c_, h):
        return acts.at[x_ * 4 + z_ * 2 + c_, h]

    def pair(x_, z_, c_, k):
        return acts.at[x_ * 4 + z_ * 2 + c_, :, k]

    def quarter(x_, z_, c_, h, k):
        return acts.at[x_ * 4 + z_ * 2 + c_, h, k]

    def push_same(ref, sends, recvs, k, dev):
        push(ref, ref, sends.at[k], recvs.at[k], dev)

    def arrived(ref, sends, recvs, k):
        remote(ref, ref, sends.at[k], recvs.at[k], sib).wait_recv()

    own = block(x, z, c)
    push_same(own, ag_send, ag_recv, 0, right)
    push_same(own, ag_send, ag_recv, 1, left)
    push_same(own, ag_send, ag_recv, 2, zdev)
    push(go.at[0], go.at[1], ex_send.at[0], ex_recv.at[0], sib)
    for u in range(8):
        push(w_cols(u, 1 - c), wt.at[1, u], ex_send.at[1 + u], ex_recv.at[1 + u], sib)
    push_same(own, sib_send, sib_recv, 0, sib)

    for load in loads[2:5]:
        load.wait()

    mine = jnp.concatenate([freq_ref[k, pl.ds(r, 1), :] for k in range(7)], axis=0)
    first = lax.broadcasted_iota(jnp.int32, (7, 128), 1) < TILE
    spread = jnp.concatenate(
        [jnp.where(first, mine[:, 2 * k : 2 * k + 1], mine[:, 2 * k + 1 : 2 * k + 2]) for k in range(16)], axis=1
    )

    def pick(k, so_far):
        row = jnp.concatenate([cos_ref[pl.ds(k, 1), :]] * 16, axis=1)
        return jnp.where(spread == k, row, so_far)

    basis[...] = lax.fori_loop(0, TILE, pick, jnp.zeros((7, 2048), F32))

    segments[...] = (
        lax.broadcasted_iota(jnp.int32, (512, 256), 0) % 256 // TILE
        == lax.broadcasted_iota(jnp.int32, (512, 256), 1) // TILE
    ).astype(F32).astype(BF16)
    chooser = (
        lax.broadcasted_iota(jnp.int32, (8, 512), 1) % 256 // TILE
        == lax.broadcasted_iota(jnp.int32, (8, 512), 0)
    ).astype(F32).astype(BF16)

    widen = (
        lax.broadcasted_iota(jnp.int32, (TILE, 16), 0) // 4 == lax.broadcasted_iota(jnp.int32, (TILE, 16), 1)
    ).astype(F32).astype(BF16)
    wide = jnp.concatenate(
        [jnp.dot(widen, freq_ref[k].astype(F32).astype(BF16), preferred_element_type=F32) for k in range(7)], axis=0
    )
    keep = (
        lax.broadcasted_iota(jnp.int32, (448, 32), 0) % 4 == lax.broadcasted_iota(jnp.int32, (448, 32), 1) % 4
    )
    narrow = (
        lax.broadcasted_iota(jnp.int32, (32, 8), 0) // 4 == lax.broadcasted_iota(jnp.int32, (32, 8), 1)
    ).astype(F32).astype(BF16)
    columns = jnp.dot(jnp.where(keep, wide, 0.0).astype(BF16), narrow, preferred_element_type=F32)
    freq_lane = lax.broadcasted_iota(jnp.int32, (448, TILE), 1).astype(F32)
    same = (
        lax.broadcasted_iota(jnp.int32, (TILE, 256), 0) % 4 == lax.broadcasted_iota(jnp.int32, (TILE, 256), 1) // TILE
    )
    for u in range(8):
        hot = (columns[:, u : u + 1] == freq_lane).astype(F32).astype(BF16)
        both = jnp.dot(hot, terms_ref[...], preferred_element_type=F32)
        for k in range(7):
            rows = both[k * TILE : (k + 1) * TILE]
            right_side[u, k, pl.ds(0, TILE), :] = jnp.where(same, rows[:, :256], 0.0).astype(BF16)
            right_side[u, k, pl.ds(TILE, TILE), :] = jnp.where(same, rows[:, 256:], 0.0).astype(BF16)

    for load in loads[5:13]:
        load.wait()
    remote(go.at[0], go.at[1], ex_send.at[0], ex_recv.at[0], sib).wait_recv()
    for u in range(8):
        remote(wt.at[0, u], wt.at[1, u], ex_send.at[1 + u], ex_recv.at[1 + u], sib).wait_recv()

    def share(dx):
        dest = (x + dx) % 4

        @pl.loop(0, 4)
        def _(k):
            rows = pl.ds(pl.multiple_of(k * 256, 256), 256)
            total = jnp.zeros((256, 256), F32)
            for part in range(2):
                pair = jnp.concatenate([wt[part, dest * 2], wt[part, dest * 2 + 1]], axis=1)
                total += jnp.dot(go[part, rows, :], pair, preferred_element_type=F32)
            q[dx, 0, rows, :] = total[:, :128]
            q[dx, 1, rows, :] = total[:, 128:]

    top, bottom = pl.ds(0, 512), pl.ds(512, 512)
    zs = (other, z)

    def encode(slot, value):
        exponents = []
        for k in range(8):
            part = value[k * TILE : (k + 1) * TILE]
            largest = jnp.max(jnp.abs(part), axis=0, keepdims=True)
            exponent = jnp.floor(jnp.log2(jnp.maximum(largest, 1e-30))) + 1.0
            whole = jnp.floor(part * (32000.0 * jnp.exp2(-exponent)) + 0.5)
            slot[pl.ds(k * TILE, TILE), :] = whole.astype(jnp.int32).astype(jnp.int16)
            exponents.append(exponent)
        tail = jnp.concatenate(exponents + [jnp.zeros((8, 128), F32)], axis=0)
        slot[pl.ds(512, 16), :] = tail.astype(jnp.int32).astype(jnp.int16)

    def decoded(slot):
        scale = jnp.exp2(slot[pl.ds(512, 16), :].astype(jnp.int32).astype(F32)) * (1.0 / 32000.0)
        return jnp.concatenate(
            [
                slot[pl.ds(k * TILE, TILE), :].astype(jnp.int32).astype(F32) * scale[k : k + 1]
                for k in range(8)
            ],
            axis=0,
        )

    def rs_push(value, direction, kind, zi):
        k = (direction * 3 + kind) * 2 + zi
        src = sx.at[direction, kind, zi]
        encode(src, value)
        push(src, rx.at[direction, kind, zi], rs_send.at[k], rs_recv.at[k], (right, left)[direction])

    def rs_wait(direction, kind, zi):
        k = (direction * 3 + kind) * 2 + zi
        slot = rx.at[direction, kind, zi]
        remote(slot, slot, rs_send.at[k], rs_recv.at[k], sib).wait_recv()
        return decoded(slot)

    def rs_first(zi):
        rs_push(q[2, zs[zi], top, :], 0, 0, zi)
        rs_push(q[2, zs[zi], bottom, :], 1, 0, zi)

    def rs_direct(zi):
        rs_push(q[1, zs[zi], bottom, :], 0, 1, zi)
        rs_push(q[3, zs[zi], top, :], 1, 1, zi)

    def rs_second(zi):
        rs_push(q[1, zs[zi], top, :] + rs_wait(0, 0, zi), 0, 2, zi)
        rs_push(q[3, zs[zi], bottom, :] + rs_wait(1, 0, zi), 1, 2, zi)

    def take(ref, k, sib_k):
        arrived(ref, ag_send, ag_recv, k)
        push_same(ref, sib_send, sib_recv, sib_k, sib)

    share(2)
    share(1)
    take(block(xl, z, c), 0, 1)
    push_same(pair(xl, z, c, 0), ag_send, ag_recv, 3, right)
    push_same(half(xl, z, c, 1), ag_send, ag_recv, 5, zdev)
    take(block(xr, z, c), 1, 2)
    push_same(pair(xr, z, c, 1), ag_send, ag_recv, 4, left)
    push_same(half(xr, z, c, 1), ag_send, ag_recv, 6, zdev)
    take(block(x, other, c), 2, 3)
    push_same(half(x, other, c, 0), ag_send, ag_recv, 9, right)
    push_same(half(x, other, c, 0), ag_send, ag_recv, 10, left)
    rs_first(0)
    share(3)
    rs_direct(0)
    share(0)
    rs_first(1)
    rs_direct(1)

    loads[13].wait()

    def unit(x_, z_):
        u = x_ * 2 + z_
        cols = pl.ds(pl.multiple_of(u * 256, 256), 256)
        both = jnp.concatenate([acts[2 * u].reshape(1024, 128), acts[2 * u + 1].reshape(1024, 128)], axis=1)
        gtmp[...] = jnp.dot(got[...], both, preferred_element_type=F32)

        @pl.loop(0, 7)
        def _(k):
            rows = pl.ds(pl.multiple_of(k * TILE, TILE), TILE)
            kept = decay_rate * mom[rows, cols] + gtmp[rows, :]
            gtmp[rows, :] = kept
            scaled = kept * basis[pl.ds(k, 1), cols]
            high = scaled.astype(BF16)
            low = (scaled - high.astype(F32)).astype(BF16)
            ycat[rows, :] = jnp.concatenate([high, low], axis=1)

        ptmp[...] = jnp.dot(ycat[...], segments[...], preferred_element_type=F32)
        lines = lax.dot_general(chooser, ycat[...], (((1,), (1,)), ((), ())), preferred_element_type=F32)
        for s_ in range(4):
            p_own[z_, pl.ds(x_ * 4 + s_, 1), :] = lines[s_ : s_ + 1]

        @pl.loop(0, 7)
        def _(k):
            rows = pl.ds(pl.multiple_of(k * TILE, TILE), TILE)
            mom[rows, cols] = gtmp[rows, :] - ptmp[rows, :] * basis[pl.ds(k, 1), cols]

        copy = pltpu.make_async_copy(mom.at[:, cols], mo_hbm.at[:, cols], store_sem.at[len(stores)])
        copy.start()
        stores.append(copy)

    stores = []
    sb = lambda x_, z_: block(x_, z_, 1 - c)
    sh = lambda x_, z_, h: half(x_, z_, 1 - c, h)

    def from_sib(ref, k):
        arrived(ref, sib_send, sib_recv, k)

    def p_zh(group, z_):
        rows = pl.ds(pl.multiple_of(z_ * 16, 16), 16)
        p_all[zh, y, rows, :] = p_own[z_]
        mine = p_all.at[zh, y, rows]
        for k, dev in enumerate(zh_devs):
            push(mine, mine, ps_send.at[group, k], ps_recv.at[group, k], dev)

    def p_y(group, z_):
        rows = pl.ds(pl.multiple_of(z_ * 16, 16), 16)
        for k in range(3):
            slot = p_all.at[(zh + 3 - k) % 4, y, rows]
            remote(slot, slot, ps_send.at[group, k], ps_recv.at[group, k], sib).wait_recv()
        mine = p_all.at[:, y, rows]
        for k, dev in enumerate(y_devs):
            push(mine, mine, py_send.at[group, k], py_recv.at[group, k], dev)

    def p_done(group, z_):
        rows = pl.ds(pl.multiple_of(z_ * 16, 16), 16)
        for k in range(3):
            slot = p_all.at[:, (y + 3 - k) % 4, rows]
            remote(slot, slot, py_send.at[group, k], py_recv.at[group, k], sib).wait_recv()

    def decode(z_):
        for h in range(2):
            tiles = p_all[:, :, pl.ds(pl.multiple_of(z_ * 16 + h * 8, 8), 8), :].reshape(8, 2, 8, 448)
            even, odd = tiles[:, 0], tiles[:, 1]
            lines = jnp.concatenate(
                [
                    jnp.concatenate([even[:, rows], odd[:, rows]], axis=1).reshape(TILE, 448)
                    for rows in (slice(0, 4), slice(4, 8))
                ],
                axis=0,
            )
            turned = jnp.transpose(lines)
            high = turned.astype(BF16)
            low = (turned - high.astype(F32)).astype(BF16)
            for k in range(2):
                own_lanes = slice(k * TILE, (k + 1) * TILE)
                lhs[k] = jnp.concatenate([high[:, own_lanes], low[:, own_lanes], high[:, own_lanes]], axis=1)
                u = (h * 2 + k) * 2 + z_
                cols = pl.ds(pl.multiple_of(u * 256, 256), 256)
                for j in range(7):
                    rows = pl.ds(j * TILE, TILE)
                    terms = right_side[u, j]
                    full = jnp.concatenate([terms[:TILE], terms], axis=0)
                    upd[rows, cols] = jnp.dot(lhs[k, rows, :], full, preferred_element_type=F32).astype(BF16)

                copy = pltpu.make_async_copy(upd.at[:, cols], up_hbm.at[:, cols], store_sem.at[len(stores)])
                copy.start()
                stores.append(copy)

    from_sib(sb(x, z), 0)
    unit(x, z)
    for k, dev_k in ((0, 3), (1, 4)):
        take(pair(xo, z, c, k), dev_k, 4 + k)
        push_same(quarter(xo, z, c, 1, k), ag_send, ag_recv, 7 + k, zdev)
    take(half(xl, other, c, 0), 9, 6)
    push_same(quarter(xl, other, c, 0, 0), ag_send, ag_recv, 11, right)
    take(half(xr, other, c, 0), 10, 7)
    push_same(quarter(xr, other, c, 0, 1), ag_send, ag_recv, 12, left)
    from_sib(sb(xl, z), 1)
    unit(xl, z)
    from_sib(sb(xr, z), 2)
    unit(xr, z)
    take(half(xl, other, c, 1), 5, 8)
    take(half(xr, other, c, 1), 6, 9)
    for k in range(2):
        from_sib(pair(xo, z, 1 - c, k), 4 + k)
    unit(xo, z)
    p_zh(0, z)
    rs_second(0)
    from_sib(sb(x, other), 3)
    unit(x, other)
    for k in range(2):
        take(quarter(xo, other, c, 0, k), 11 + k, 10 + k)
        take(quarter(xo, other, c, 1, k), 7 + k, 12 + k)
    from_sib(sh(xl, other, 0), 6)
    from_sib(sh(xl, other, 1), 8)
    unit(xl, other)
    p_y(0, z)
    from_sib(sh(xr, other, 0), 7)
    from_sib(sh(xr, other, 1), 9)
    unit(xr, other)
    for k in range(2):
        from_sib(quarter(xo, other, 1 - c, 0, k), 10 + k)
        from_sib(quarter(xo, other, 1 - c, 1, k), 12 + k)
    unit(xo, other)
    p_zh(1, other)
    rs_second(1)

    def x_sum(zi):
        return (
            q[0, zs[zi], top, :] + rs_wait(0, 2, zi) + rs_wait(1, 1, zi),
            q[0, zs[zi], bottom, :] + rs_wait(0, 1, zi) + rs_wait(1, 2, zi),
        )

    for k, value in enumerate(x_sum(0)):
        encode(sz.at[k], value)
    push(sz, rz, zs_send, zs_recv, zdev)
    p_y(1, other)
    p_done(0, z)
    decode(z)
    p_done(1, other)
    decode(other)

    sums = x_sum(1)
    remote(sz, rz, zs_send, zs_recv, zdev).wait_recv()
    for k in range(2):
        ig[pl.ds(k * 512, 512), :] = (sums[k] + decoded(rz.at[k])).astype(BF16)
    last = pltpu.make_async_copy(ig, ig_hbm, store_sem.at[len(stores)])
    last.start()
    for copy in stores:
        copy.wait()
    last.wait()
    for copy in sent:
        copy.wait_send()


def body(activations, grad_out, weight, momentum, freq_rows):
    hbm = pl.BlockSpec(memory_space=pltpu.HBM)
    dma = pltpu.SemaphoreType.DMA
    table, terms = cosine_tables()
    input_grad, momentum_out, update = pl.pallas_call(
        kernel,
        out_shape=(
            jax.ShapeDtypeStruct((1024, 128), BF16),
            jax.ShapeDtypeStruct((448, 2048), F32),
            jax.ShapeDtypeStruct((448, 2048), BF16),
        ),
        in_specs=[hbm] * 7,
        out_specs=(hbm, hbm, hbm),
        scratch_shapes=[
            pltpu.VMEM((16, 2, 2, 256, 128), BF16),
            pltpu.VMEM((448, 1024), BF16),
            pltpu.VMEM((2, 1024, 448), BF16),
            pltpu.VMEM((2, 8, 448, 128), BF16),
            pltpu.VMEM((4, 2, 1024, 128), F32),
            pltpu.VMEM((2, 3, 2, 528, 128), jnp.int16),
            pltpu.VMEM((2, 3, 2, 528, 128), jnp.int16),
            pltpu.VMEM((2, 528, 128), jnp.int16),
            pltpu.VMEM((2, 528, 128), jnp.int16),
            pltpu.VMEM((448, 2048), F32),
            pltpu.VMEM((448, 256), F32),
            pltpu.VMEM((448, 256), F32),
            pltpu.VMEM((448, 512), BF16),
            pltpu.VMEM((7, 2048), F32),
            pltpu.VMEM((512, 256), BF16),
            pltpu.VMEM((8, 7, 128, 256), BF16),
            pltpu.VMEM((2, 448, 192), BF16),
            pltpu.VMEM((2, 16, 448), F32),
            pltpu.VMEM((4, 4, 32, 448), F32),
            pltpu.VMEM((448, 2048), BF16),
            pltpu.VMEM((1024, 128), BF16),
            pltpu.VMEM((7, 16, 32), jnp.int32),
            pltpu.VMEM((TILE, 128), F32),
            pltpu.VMEM((TILE, 512), BF16),
            dma((14,)), dma((17,)),
            dma((9,)), dma((9,)),
            dma((13,)), dma((13,)),
            dma((14,)), dma((14,)),
            dma((12,)), dma((12,)),
            dma, dma,
            dma((2, 3)), dma((2, 3)),
            dma((2, 3)), dma((2, 3)),
        ],
        compiler_params=pltpu.CompilerParams(
            collective_id=0, has_side_effects=True, vmem_limit_bytes=63 * 1024 * 1024
        ),
        name="demo_step",
    )(
        activations.reshape(2, 2, 256, 128),
        grad_out.T,
        weight.T,
        momentum[0].T,
        freq_rows.transpose(2, 0, 1),
        jnp.asarray(table),
        jnp.asarray(terms),
    )
    return input_grad, momentum_out.T[None], update.T


def solution(mesh):
    placed = (
        P("replica", "tensor"),
        P("replica", "tensor"),
        P(None, "tensor"),
        P("replica", None, "tensor"),
        P(None, None, "tensor"),
    )
    return jax.shard_map(
        body,
        mesh=mesh,
        in_specs=placed,
        out_specs=(P("replica", "tensor"), P("replica", None, "tensor"), P(None, "tensor")),
        check_vma=False,
    )
```

time: 87.9 us -> 65.7 us (0.75)
  local copies, waits for them, and re-layouts: 19.9 us -> 7.34 us
  Pallas kernels: 66.8 us -> 57.6 us
    unnamed x13 -> x5, local copies, waits for them, and re-layouts: 19.9 us -> 7.34 us
    pallas_call x1, Pallas kernels: 66.8 us -> 57.6 us  [body(): pl.pallas_call(kernel, out_shape=(jax.ShapeDtypeStruct((1024, 128), BF16)...]
where the time goes in v2:
time: 65.7 us; the launch traced here: 65.6 us
  Pallas kernels  57.6 us (88%)
  local copies, waits for them, and re-layouts  7.34 us (11%)
    pallas_call x1, Pallas kernels, body(): pl.pallas_call(kernel, out_shape=(jax.ShapeDtypeStruct((1024, 128), BF16)...  57.6 us
    unnamed x5, local copies, waits for them, and re-layouts  7.34 us

profile of v2, /device:TPU:2, one launch (start us, length us, event | category | flops | bytes accessed | tf_op | source)
XLA Modules:
  0.0 65.6 jit_solution(13284277561804765637)
XLA Ops:
  0.6 57.6 %demo_step.1 = (bf16[1024,128]{1,0:T(8,128)(2,1)}, f32[448,2048]{1,0:T(8,128)}, bf16[448,2048]{1,0:T(8,128)(2,1)}) custom-call(bf16[2,2,256,128]{3,2,1,0:T(8,128)(2,1)} %bitcast.16, bf16[448,1024]{1,0:T(8,128)(2,1)} %bitcast.15, bf16[448,2048]{1,0:T(8,128)(2,1)} %bitcast.14, f32[448,2048]{1,0:T(8,128)} %bitcast.12, s32[7,16,32]{2,1,0:T(8,128)} %bitcast.17, ...), custom_call_target="tpu_custom_call" | custom-call | tf_op jit(solution)/shard_map/demo_step/pallas_call | solution.py:415
  58.2 1.7 %copy.13 = bf16[1024,128]{1,0:T(8,128)(2,1)} copy(bf16[1024,128]{1,0:T(8,128)(2,1)} %get-tuple-element.12) | data formatting | bytes 524288
  59.9 0.0 copy-start
  59.9 4.4 %copy.14 = f32[1,2048,448]{1,2,0:T(8,128)} copy(f32[1,2048,448]{1,2,0:T(8,128)} %bitcast.11) | data formatting | bytes 7340032
  64.3 0.0 copy-done
  64.3 1.2 %copy.15 = bf16[2048,448]{0,1:T(8,128)(2,1)} copy(bf16[2048,448]{0,1:T(8,128)(2,1)S(1)} %bitcast.13) | data formatting | bytes 3670016
Async XLA Ops:
  59.9 4.4 %copy-start = (bf16[448,2048]{1,0:T(8,128)(2,1)S(1)}, bf16[448,2048]{1,0:T(8,128)(2,1)}, u32[]{:S(2)}) copy-start(bf16[448,2048]{1,0:T(8,128)(2,1)} %get-tuple-element.8) | copy-start | bytes 5505028

commit v3 on v2

--- a/solution.py
+++ b/solution.py
@@ -28,10 +28,10 @@
 
 def kernel(
     act_hbm, go_hbm, w_hbm, mom_hbm, freq_hbm, cos_hbm, terms_hbm,
-    ig_hbm, mo_hbm, up_hbm,
-    acts, got, go, wt, q, sx, rx, sz, rz, mom, gtmp, ptmp, ycat, basis, segments, right_side, lhs, p_own, p_all, upd, ig,
+    ig, mom, upd,
+    acts, got, go, wt, q, sx, rx, sz, rz, gtmp, ptmp, ycat, basis, segments, right_side, lhs, p_own, p_all,
     freq_ref, cos_ref, terms_ref,
-    load_sem, store_sem, ex_send, ex_recv, ag_send, ag_recv, sib_send, sib_recv,
+    load_sem, ex_send, ex_recv, ag_send, ag_recv, sib_send, sib_recv,
     rs_send, rs_recv, zs_send, zs_recv, ps_send, ps_recv, py_send, py_recv,
 ):
     r = lax.axis_index("replica")
@@ -91,9 +91,6 @@
     def half(x_, z_, c_, h):
         return acts.at[x_ * 4 + z_ * 2 + c_, h]
 
-    def pair(x_, z_, c_, k):
-        return acts.at[x_ * 4 + z_ * 2 + c_, :, k]
-
     def quarter(x_, z_, c_, h, k):
         return acts.at[x_ * 4 + z_ * 2 + c_, h, k]
 
@@ -103,14 +100,19 @@
     def arrived(ref, sends, recvs, k):
         remote(ref, ref, sends.at[k], recvs.at[k], sib).wait_recv()
 
-    own = block(x, z, c)
-    push_same(own, ag_send, ag_recv, 0, right)
-    push_same(own, ag_send, ag_recv, 1, left)
-    push_same(own, ag_send, ag_recv, 2, zdev)
+    def own(h):
+        return half(x, z, c, h)
+
+    push_same(own(1), ag_send, ag_recv, 0, right)
+    push_same(own(1), ag_send, ag_recv, 1, left)
+    push_same(own(0), ag_send, ag_recv, 2, zdev)
+    push_same(own(0), ag_send, ag_recv, 3, right)
+    push_same(own(0), ag_send, ag_recv, 4, left)
+    push_same(own(1), ag_send, ag_recv, 5, zdev)
     push(go.at[0], go.at[1], ex_send.at[0], ex_recv.at[0], sib)
     for u in range(8):
         push(w_cols(u, 1 - c), wt.at[1, u], ex_send.at[1 + u], ex_recv.at[1 + u], sib)
-    push_same(own, sib_send, sib_recv, 0, sib)
+    push_same(block(x, z, c), sib_send, sib_recv, 0, sib)
 
     for load in loads[2:5]:
         load.wait()
@@ -160,6 +162,20 @@
             rows = both[k * TILE : (k + 1) * TILE]
             right_side[u, k, pl.ds(0, TILE), :] = jnp.where(same, rows[:, :256], 0.0).astype(BF16)
             right_side[u, k, pl.ds(TILE, TILE), :] = jnp.where(same, rows[:, 256:], 0.0).astype(BF16)
+
+    def take(ref, k, sib_k):
+        arrived(ref, ag_send, ag_recv, k)
+        push_same(ref, sib_send, sib_recv, sib_k, sib)
+
+    take(half(xl, z, c, 1), 0, 1)
+    push_same(half(xl, z, c, 1), ag_send, ag_recv, 6, zdev)
+    push_same(quarter(xl, z, c, 1, 0), ag_send, ag_recv, 7, right)
+    take(half(xr, z, c, 1), 1, 2)
+    push_same(half(xr, z, c, 1), ag_send, ag_recv, 8, zdev)
+    push_same(quarter(xr, z, c, 1, 1), ag_send, ag_recv, 9, left)
+    take(half(x, other, c, 0), 2, 3)
+    push_same(half(x, other, c, 0), ag_send, ag_recv, 10, right)
+    push_same(half(x, other, c, 0), ag_send, ag_recv, 11, left)
 
     for load in loads[5:13]:
         load.wait()
@@ -229,23 +245,23 @@
         rs_push(q[1, zs[zi], top, :] + rs_wait(0, 0, zi), 0, 2, zi)
         rs_push(q[3, zs[zi], bottom, :] + rs_wait(1, 0, zi), 1, 2, zi)
 
-    def take(ref, k, sib_k):
-        arrived(ref, ag_send, ag_recv, k)
-        push_same(ref, sib_send, sib_recv, sib_k, sib)
-
     share(2)
+    take(half(xl, z, c, 0), 3, 4)
+    push_same(quarter(xl, z, c, 0, 0), ag_send, ag_recv, 12, right)
+    take(half(xr, z, c, 0), 4, 5)
+    push_same(quarter(xr, z, c, 0, 1), ag_send, ag_recv, 13, left)
+    take(half(x, other, c, 1), 5, 6)
+    rs_first(0)
     share(1)
-    take(block(xl, z, c), 0, 1)
-    push_same(pair(xl, z, c, 0), ag_send, ag_recv, 3, right)
-    push_same(half(xl, z, c, 1), ag_send, ag_recv, 5, zdev)
-    take(block(xr, z, c), 1, 2)
-    push_same(pair(xr, z, c, 1), ag_send, ag_recv, 4, left)
-    push_same(half(xr, z, c, 1), ag_send, ag_recv, 6, zdev)
-    take(block(x, other, c), 2, 3)
-    push_same(half(x, other, c, 0), ag_send, ag_recv, 9, right)
-    push_same(half(x, other, c, 0), ag_send, ag_recv, 10, left)
-    rs_first(0)
     share(3)
+    take(quarter(xo, z, c, 1, 0), 7, 7)
+    push_same(quarter(xo, z, c, 1, 0), ag_send, ag_recv, 14, zdev)
+    take(quarter(xo, z, c, 1, 1), 9, 8)
+    push_same(quarter(xo, z, c, 1, 1), ag_send, ag_recv, 15, zdev)
+    take(half(xl, other, c, 0), 10, 9)
+    push_same(quarter(xl, other, c, 0, 0), ag_send, ag_recv, 16, right)
+    take(half(xr, other, c, 0), 11, 10)
+    push_same(quarter(xr, other, c, 0, 1), ag_send, ag_recv, 17, left)
     rs_direct(0)
     share(0)
     rs_first(1)
@@ -253,132 +269,121 @@
 
     loads[13].wait()
 
-    def unit(x_, z_):
+    def unit(dx, x_, z_, zi):
         u = x_ * 2 + z_
         cols = pl.ds(pl.multiple_of(u * 256, 256), 256)
         both = jnp.concatenate([acts[2 * u].reshape(1024, 128), acts[2 * u + 1].reshape(1024, 128)], axis=1)
         gtmp[...] = jnp.dot(got[...], both, preferred_element_type=F32)
 
-        @pl.loop(0, 7)
-        def _(k):
-            rows = pl.ds(pl.multiple_of(k * TILE, TILE), TILE)
+        for k in range(7):
+            rows = pl.ds(k * TILE, TILE)
             kept = decay_rate * mom[rows, cols] + gtmp[rows, :]
             gtmp[rows, :] = kept
-            scaled = kept * basis[pl.ds(k, 1), cols]
+            scaled = kept * basis[k : k + 1, cols]
             high = scaled.astype(BF16)
             low = (scaled - high.astype(F32)).astype(BF16)
             ycat[rows, :] = jnp.concatenate([high, low], axis=1)
 
         ptmp[...] = jnp.dot(ycat[...], segments[...], preferred_element_type=F32)
         lines = lax.dot_general(chooser, ycat[...], (((1,), (1,)), ((), ())), preferred_element_type=F32)
-        for s_ in range(4):
-            p_own[z_, pl.ds(x_ * 4 + s_, 1), :] = lines[s_ : s_ + 1]
-
-        @pl.loop(0, 7)
-        def _(k):
-            rows = pl.ds(pl.multiple_of(k * TILE, TILE), TILE)
-            mom[rows, cols] = gtmp[rows, :] - ptmp[rows, :] * basis[pl.ds(k, 1), cols]
-
-        copy = pltpu.make_async_copy(mom.at[:, cols], mo_hbm.at[:, cols], store_sem.at[len(stores)])
-        copy.start()
-        stores.append(copy)
-
-    stores = []
+        p_own[zi, dx // 2, pl.ds(dx % 2 * 4, 4), :] = lines[:4]
+        for k in range(7):
+            rows = pl.ds(k * TILE, TILE)
+            mom[rows, cols] = gtmp[rows, :] - ptmp[rows, :] * basis[k : k + 1, cols]
+
     sb = lambda x_, z_: block(x_, z_, 1 - c)
     sh = lambda x_, z_, h: half(x_, z_, 1 - c, h)
 
     def from_sib(ref, k):
         arrived(ref, sib_send, sib_recv, k)
 
-    def p_zh(group, z_):
-        rows = pl.ds(pl.multiple_of(z_ * 16, 16), 16)
-        p_all[zh, y, rows, :] = p_own[z_]
-        mine = p_all.at[zh, y, rows]
+    xs = (x, xl, xr, xo)
+
+    def p_zh(group):
+        p_all[group, zh, y] = p_own[group // 2, group % 2]
+        mine = p_all.at[group, zh, y]
         for k, dev in enumerate(zh_devs):
             push(mine, mine, ps_send.at[group, k], ps_recv.at[group, k], dev)
 
-    def p_y(group, z_):
-        rows = pl.ds(pl.multiple_of(z_ * 16, 16), 16)
+    def p_y(group):
         for k in range(3):
-            slot = p_all.at[(zh + 3 - k) % 4, y, rows]
+            slot = p_all.at[group, (zh + 3 - k) % 4, y]
             remote(slot, slot, ps_send.at[group, k], ps_recv.at[group, k], sib).wait_recv()
-        mine = p_all.at[:, y, rows]
+        mine = p_all.at[group, :, y]
         for k, dev in enumerate(y_devs):
             push(mine, mine, py_send.at[group, k], py_recv.at[group, k], dev)
 
-    def p_done(group, z_):
-        rows = pl.ds(pl.multiple_of(z_ * 16, 16), 16)
+    def finish(group):
         for k in range(3):
-            slot = p_all.at[:, (y + 3 - k) % 4, rows]
+            slot = p_all.at[group, :, (y + 3 - k) % 4]
             remote(slot, slot, py_send.at[group, k], py_recv.at[group, k], sib).wait_recv()
-
-    def decode(z_):
-        for h in range(2):
-            tiles = p_all[:, :, pl.ds(pl.multiple_of(z_ * 16 + h * 8, 8), 8), :].reshape(8, 2, 8, 448)
-            even, odd = tiles[:, 0], tiles[:, 1]
-            lines = jnp.concatenate(
-                [
-                    jnp.concatenate([even[:, rows], odd[:, rows]], axis=1).reshape(TILE, 448)
-                    for rows in (slice(0, 4), slice(4, 8))
-                ],
-                axis=0,
-            )
-            turned = jnp.transpose(lines)
-            high = turned.astype(BF16)
-            low = (turned - high.astype(F32)).astype(BF16)
-            for k in range(2):
-                own_lanes = slice(k * TILE, (k + 1) * TILE)
-                lhs[k] = jnp.concatenate([high[:, own_lanes], low[:, own_lanes], high[:, own_lanes]], axis=1)
-                u = (h * 2 + k) * 2 + z_
-                cols = pl.ds(pl.multiple_of(u * 256, 256), 256)
-                for j in range(7):
-                    rows = pl.ds(j * TILE, TILE)
-                    terms = right_side[u, j]
-                    full = jnp.concatenate([terms[:TILE], terms], axis=0)
-                    upd[rows, cols] = jnp.dot(lhs[k, rows, :], full, preferred_element_type=F32).astype(BF16)
-
-                copy = pltpu.make_async_copy(upd.at[:, cols], up_hbm.at[:, cols], store_sem.at[len(stores)])
-                copy.start()
-                stores.append(copy)
+        tiles = p_all[group].reshape(8, 2, 8, 448)
+        even, odd = tiles[:, 0], tiles[:, 1]
+        lines = jnp.concatenate(
+            [
+                jnp.concatenate([even[:, rows], odd[:, rows]], axis=1).reshape(TILE, 448)
+                for rows in (slice(0, 4), slice(4, 8))
+            ],
+            axis=0,
+        )
+        turned = jnp.transpose(lines)
+        high = turned.astype(BF16)
+        low = (turned - high.astype(F32)).astype(BF16)
+        for k in range(2):
+            own_lanes = slice(k * TILE, (k + 1) * TILE)
+            lhs[k] = jnp.concatenate([high[:, own_lanes], low[:, own_lanes], high[:, own_lanes]], axis=1)
+            u = xs[group % 2 * 2 + k] * 2 + (z, other)[group // 2]
+            cols = pl.ds(pl.multiple_of(u * 256, 256), 256)
+            for j in range(7):
+                rows = pl.ds(j * TILE, TILE)
+                terms = right_side[u, j]
+                full = jnp.concatenate([terms[:TILE], terms], axis=0)
+                upd[rows, cols] = jnp.dot(lhs[k, rows, :], full, preferred_element_type=F32).astype(BF16)
 
     from_sib(sb(x, z), 0)
-    unit(x, z)
-    for k, dev_k in ((0, 3), (1, 4)):
-        take(pair(xo, z, c, k), dev_k, 4 + k)
-        push_same(quarter(xo, z, c, 1, k), ag_send, ag_recv, 7 + k, zdev)
-    take(half(xl, other, c, 0), 9, 6)
-    push_same(quarter(xl, other, c, 0, 0), ag_send, ag_recv, 11, right)
-    take(half(xr, other, c, 0), 10, 7)
-    push_same(quarter(xr, other, c, 0, 1), ag_send, ag_recv, 12, left)
-    from_sib(sb(xl, z), 1)
-    unit(xl, z)
-    from_sib(sb(xr, z), 2)
-    unit(xr, z)
-    take(half(xl, other, c, 1), 5, 8)
-    take(half(xr, other, c, 1), 6, 9)
-    for k in range(2):
-        from_sib(pair(xo, z, 1 - c, k), 4 + k)
-    unit(xo, z)
-    p_zh(0, z)
+    unit(0, x, z, 0)
+    from_sib(sh(xl, z, 1), 1)
+    from_sib(sh(xl, z, 0), 4)
+    unit(1, xl, z, 0)
+    p_zh(0)
+    take(quarter(xo, z, c, 0, 0), 12, 11)
+    take(quarter(xo, z, c, 0, 1), 13, 12)
+    take(half(xl, other, c, 1), 6, 13)
+    take(half(xr, other, c, 1), 8, 14)
+    from_sib(sh(xr, z, 1), 2)
+    from_sib(sh(xr, z, 0), 5)
+    unit(2, xr, z, 0)
+    from_sib(quarter(xo, z, 1 - c, 1, 0), 7)
+    from_sib(quarter(xo, z, 1 - c, 1, 1), 8)
+    from_sib(quarter(xo, z, 1 - c, 0, 0), 11)
+    from_sib(quarter(xo, z, 1 - c, 0, 1), 12)
+    unit(3, xo, z, 0)
+    p_zh(1)
     rs_second(0)
-    from_sib(sb(x, other), 3)
-    unit(x, other)
-    for k in range(2):
-        take(quarter(xo, other, c, 0, k), 11 + k, 10 + k)
-        take(quarter(xo, other, c, 1, k), 7 + k, 12 + k)
-    from_sib(sh(xl, other, 0), 6)
-    from_sib(sh(xl, other, 1), 8)
-    unit(xl, other)
-    p_y(0, z)
-    from_sib(sh(xr, other, 0), 7)
-    from_sib(sh(xr, other, 1), 9)
-    unit(xr, other)
-    for k in range(2):
-        from_sib(quarter(xo, other, 1 - c, 0, k), 10 + k)
-        from_sib(quarter(xo, other, 1 - c, 1, k), 12 + k)
-    unit(xo, other)
-    p_zh(1, other)
+    from_sib(sh(x, other, 0), 3)
+    from_sib(sh(x, other, 1), 6)
+    unit(0, x, other, 1)
+    take(quarter(xo, other, c, 0, 0), 16, 15)
+    take(quarter(xo, other, c, 0, 1), 17, 16)
+    take(quarter(xo, other, c, 1, 0), 14, 17)
+    take(quarter(xo, other, c, 1, 1), 15, 18)
+    p_y(0)
+    from_sib(sh(xl, other, 0), 9)
+    from_sib(sh(xl, other, 1), 13)
+    unit(1, xl, other, 1)
+    p_zh(2)
+    p_y(1)
+    from_sib(sh(xr, other, 0), 10)
+    from_sib(sh(xr, other, 1), 14)
+    unit(2, xr, other, 1)
+    from_sib(quarter(xo, other, 1 - c, 0, 0), 15)
+    from_sib(quarter(xo, other, 1 - c, 0, 1), 16)
+    from_sib(quarter(xo, other, 1 - c, 1, 0), 17)
+    from_sib(quarter(xo, other, 1 - c, 1, 1), 18)
+    unit(3, xo, other, 1)
+    p_zh(3)
     rs_second(1)
+    p_y(2)
 
     def x_sum(zi):
         return (
@@ -389,38 +394,49 @@
     for k, value in enumerate(x_sum(0)):
         encode(sz.at[k], value)
     push(sz, rz, zs_send, zs_recv, zdev)
-    p_y(1, other)
-    p_done(0, z)
-    decode(z)
-    p_done(1, other)
-    decode(other)
+    finish(0)
+    p_y(3)
+    finish(1)
+    finish(2)
+    finish(3)
 
     sums = x_sum(1)
     remote(sz, rz, zs_send, zs_recv, zdev).wait_recv()
     for k in range(2):
         ig[pl.ds(k * 512, 512), :] = (sums[k] + decoded(rz.at[k])).astype(BF16)
-    last = pltpu.make_async_copy(ig, ig_hbm, store_sem.at[len(stores)])
-    last.start()
-    for copy in stores:
-        copy.wait()
-    last.wait()
     for copy in sent:
         copy.wait_send()
 
 
+def store(*refs):
+    sources, targets, sems = refs[:3], refs[3:6], refs[6]
+    copies = []
+    for k, (source, target) in enumerate(zip(sources, targets)):
+        height = source.shape[0] // 4
+        for part in range(4):
+            rows = pl.ds(part * height, height)
+            copies.append(pltpu.make_async_copy(source.at[rows], target.at[rows], sems.at[k, part]))
+    for copy in copies:
+        copy.start()
+    for copy in copies:
+        copy.wait()
+
+
 def body(activations, grad_out, weight, momentum, freq_rows):
     hbm = pl.BlockSpec(memory_space=pltpu.HBM)
+    vmem = pl.BlockSpec(memory_space=pltpu.VMEM)
     dma = pltpu.SemaphoreType.DMA
+    outs = (
+        jax.ShapeDtypeStruct((1024, 128), BF16),
+        jax.ShapeDtypeStruct((448, 2048), F32),
+        jax.ShapeDtypeStruct((448, 2048), BF16),
+    )
     table, terms = cosine_tables()
     input_grad, momentum_out, update = pl.pallas_call(
         kernel,
-        out_shape=(
-            jax.ShapeDtypeStruct((1024, 128), BF16),
-            jax.ShapeDtypeStruct((448, 2048), F32),
-            jax.ShapeDtypeStruct((448, 2048), BF16),
-        ),
+        out_shape=outs,
         in_specs=[hbm] * 7,
-        out_specs=(hbm, hbm, hbm),
+        out_specs=(vmem, vmem, vmem),
         scratch_shapes=[
             pltpu.VMEM((16, 2, 2, 256, 128), BF16),
             pltpu.VMEM((448, 1024), BF16),
@@ -431,7 +447,6 @@
             pltpu.VMEM((2, 3, 2, 528, 128), jnp.int16),
             pltpu.VMEM((2, 528, 128), jnp.int16),
             pltpu.VMEM((2, 528, 128), jnp.int16),
-            pltpu.VMEM((448, 2048), F32),
             pltpu.VMEM((448, 256), F32),
             pltpu.VMEM((448, 256), F32),
             pltpu.VMEM((448, 512), BF16),
@@ -439,35 +454,47 @@
             pltpu.VMEM((512, 256), BF16),
             pltpu.VMEM((8, 7, 128, 256), BF16),
             pltpu.VMEM((2, 448, 192), BF16),
-            pltpu.VMEM((2, 16, 448), F32),
-            pltpu.VMEM((4, 4, 32, 448), F32),
-            pltpu.VMEM((448, 2048), BF16),
-            pltpu.VMEM((1024, 128), BF16),
+            pltpu.VMEM((2, 2, 8, 448), F32),
+            pltpu.VMEM((4, 4, 4, 8, 448), F32),
             pltpu.VMEM((7, 16, 32), jnp.int32),
             pltpu.VMEM((TILE, 128), F32),
             pltpu.VMEM((TILE, 512), BF16),
-            dma((14,)), dma((17,)),
+            dma((14,)),
             dma((9,)), dma((9,)),
-            dma((13,)), dma((13,)),
-            dma((14,)), dma((14,)),
+            dma((18,)), dma((18,)),
+            dma((19,)), dma((19,)),
             dma((12,)), dma((12,)),
             dma, dma,
-            dma((2, 3)), dma((2, 3)),
-            dma((2, 3)), dma((2, 3)),
+            dma((4, 3)), dma((4, 3)),
+            dma((4, 3)), dma((4, 3)),
         ],
         compiler_params=pltpu.CompilerParams(
-            collective_id=0, has_side_effects=True, vmem_limit_bytes=63 * 1024 * 1024
+            collective_id=0, has_side_effects=True, vmem_limit_bytes=40 * 1024 * 1024
         ),
         name="demo_step",
     )(
-        activations.reshape(2, 2, 256, 128),
-        grad_out.T,
-        weight.T,
-        momentum[0].T,
-        freq_rows.transpose(2, 0, 1),
-        jnp.asarray(table),
-        jnp.asarray(terms),
-    )
+        *(
+            pltpu.with_memory_space_constraint(value, pltpu.HBM)
+            for value in (
+                activations.reshape(2, 2, 256, 128),
+                grad_out.T,
+                weight.T,
+                momentum[0].T,
+                freq_rows.transpose(2, 0, 1),
+                jnp.asarray(table),
+                jnp.asarray(terms),
+            )
+        )
+    )
+    input_grad, momentum_out, update = pl.pallas_call(
+        store,
+        out_shape=outs,
+        in_specs=[pl.BlockSpec(memory_space=pl.ANY)] * 3,
+        out_specs=(hbm, hbm, hbm),
+        scratch_shapes=[dma((3, 4))],
+        compiler_params=pltpu.CompilerParams(vmem_limit_bytes=4 * 1024 * 1024),
+        name="store_results",
+    )(*(pltpu.with_memory_space_constraint(value, pltpu.VMEM) for value in (input_grad, momentum_out, update)))
     return input_grad, momentum_out.T[None], update.T
 
 

time: 65.7 us -> 51.7 us (0.79)
  local copies, waits for them, and re-layouts: 7.34 us -> 0 us
  Pallas kernels: 57.6 us -> 51 us
    unnamed x5 -> x0, local copies, waits for them, and re-layouts: 7.34 us -> none
    pallas_call x1 -> x2, Pallas kernels: 57.6 us -> 51 us  [the longest x1 48.4 us: body(): pl.pallas_call(kernel, out_shape=outs, in_specs=[hbm] * 7, out_specs=(vme...]
where the time goes in v3:
time: 51.7 us; the launch traced here: 51.6 us
  Pallas kernels  51 us (99%)
  between operations  0.64 us (1%)
    pallas_call x1, Pallas kernels, body(): pl.pallas_call(kernel, out_shape=outs, in_specs=[hbm] * 7, out_specs=(vme...  48.4 us
    pallas_call x1, Pallas kernels, body(): pl.pallas_call(store, out_shape=outs, in_specs=[pl.BlockSpec(memory_space...  2.6 us

profile of v3, /device:TPU:2, one launch (start us, length us, event | category | flops | bytes accessed | tf_op | source)
XLA Modules:
  0.0 51.6 jit_solution(6478045149585746072)
XLA Ops:
  0.6 48.4 %demo_step.1 = (bf16[1024,128]{1,0:T(8,128)(2,1)S(1)}, f32[448,2048]{1,0:T(8,128)S(1)}, bf16[448,2048]{1,0:T(8,128)(2,1)S(1)}) custom-call(bf16[2,2,256,128]{3,2,1,0:T(8,128)(2,1)} %bitcast.14, bf16[448,1024]{1,0:T(8,128)(2,1)} %bitcast.13, bf16[448,2048]{1,0:T(8,128)(2,1)} %bitcast.12, f32[448,2048]{1,0:T(8,128)} %bitcast.11, s32[7,16,32]{2,1,0:T(8,128)} %bitcast.15, ...), custom_call_target="tpu_custom_call" | custom-call | tf_op jit(solution)/shard_map/demo_step/pallas_call | solution.py:435
  49.0 2.6 %store_results.1 = (bf16[1024,128]{1,0:T(8,128)(2,1)}, f32[448,2048]{1,0:T(8,128)}, bf16[448,2048]{1,0:T(8,128)(2,1)}) custom-call(bf16[1024,128]{1,0:T(8,128)(2,1)S(1)} %get-tuple-element.9.refs_0_, f32[448,2048]{1,0:T(8,128)S(1)} %get-tuple-element.10.refs_1_, bf16[448,2048]{1,0:T(8,128)(2,1)S(1)} %get-tuple-element.11.refs_2_), custom_call_target="tpu_custom_call" | custom-call | tf_op jit(solution)/shard_map/store_results/pallas_call | solution.py:489

commit v4 on v3

--- a/solution.py
+++ b/solution.py
@@ -264,8 +264,6 @@
     push_same(quarter(xr, other, c, 0, 1), ag_send, ag_recv, 17, left)
     rs_direct(0)
     share(0)
-    rs_first(1)
-    rs_direct(1)
 
     loads[13].wait()
 
@@ -342,14 +340,14 @@
 
     from_sib(sb(x, z), 0)
     unit(0, x, z, 0)
+    take(quarter(xo, z, c, 0, 0), 12, 11)
+    take(quarter(xo, z, c, 0, 1), 13, 12)
+    take(half(xl, other, c, 1), 6, 13)
+    take(half(xr, other, c, 1), 8, 14)
     from_sib(sh(xl, z, 1), 1)
     from_sib(sh(xl, z, 0), 4)
     unit(1, xl, z, 0)
     p_zh(0)
-    take(quarter(xo, z, c, 0, 0), 12, 11)
-    take(quarter(xo, z, c, 0, 1), 13, 12)
-    take(half(xl, other, c, 1), 6, 13)
-    take(half(xr, other, c, 1), 8, 14)
     from_sib(sh(xr, z, 1), 2)
     from_sib(sh(xr, z, 0), 5)
     unit(2, xr, z, 0)
@@ -360,13 +358,15 @@
     unit(3, xo, z, 0)
     p_zh(1)
     rs_second(0)
-    from_sib(sh(x, other, 0), 3)
-    from_sib(sh(x, other, 1), 6)
-    unit(0, x, other, 1)
+    rs_first(1)
+    rs_direct(1)
     take(quarter(xo, other, c, 0, 0), 16, 15)
     take(quarter(xo, other, c, 0, 1), 17, 16)
     take(quarter(xo, other, c, 1, 0), 14, 17)
     take(quarter(xo, other, c, 1, 1), 15, 18)
+    from_sib(sh(x, other, 0), 3)
+    from_sib(sh(x, other, 1), 6)
+    unit(0, x, other, 1)
     p_y(0)
     from_sib(sh(xl, other, 0), 9)
     from_sib(sh(xl, other, 1), 13)
@@ -382,9 +382,7 @@
     from_sib(quarter(xo, other, 1 - c, 1, 1), 18)
     unit(3, xo, other, 1)
     p_zh(3)
-    rs_second(1)
     p_y(2)
-
     def x_sum(zi):
         return (
             q[0, zs[zi], top, :] + rs_wait(0, 2, zi) + rs_wait(1, 1, zi),
@@ -393,16 +391,18 @@
 
     for k, value in enumerate(x_sum(0)):
         encode(sz.at[k], value)
-    push(sz, rz, zs_send, zs_recv, zdev)
+        push(sz.at[k], rz.at[k], zs_send.at[k], zs_recv.at[k], zdev)
+    rs_second(1)
+
+    p_y(3)
     finish(0)
-    p_y(3)
     finish(1)
     finish(2)
     finish(3)
 
     sums = x_sum(1)
-    remote(sz, rz, zs_send, zs_recv, zdev).wait_recv()
     for k in range(2):
+        remote(sz.at[k], rz.at[k], zs_send.at[k], zs_recv.at[k], zdev).wait_recv()
         ig[pl.ds(k * 512, 512), :] = (sums[k] + decoded(rz.at[k])).astype(BF16)
     for copy in sent:
         copy.wait_send()
@@ -412,8 +412,9 @@
     sources, targets, sems = refs[:3], refs[3:6], refs[6]
     copies = []
     for k, (source, target) in enumerate(zip(sources, targets)):
-        height = source.shape[0] // 4
-        for part in range(4):
+        parts = 7 if source.shape[0] == 448 else 4
+        height = source.shape[0] // parts
+        for part in range(parts):
             rows = pl.ds(part * height, height)
             copies.append(pltpu.make_async_copy(source.at[rows], target.at[rows], sems.at[k, part]))
     for copy in copies:
@@ -464,7 +465,7 @@
             dma((18,)), dma((18,)),
             dma((19,)), dma((19,)),
             dma((12,)), dma((12,)),
-            dma, dma,
+            dma((2,)), dma((2,)),
             dma((4, 3)), dma((4, 3)),
             dma((4, 3)), dma((4, 3)),
         ],
@@ -491,7 +492,7 @@
         out_shape=outs,
         in_specs=[pl.BlockSpec(memory_space=pl.ANY)] * 3,
         out_specs=(hbm, hbm, hbm),
-        scratch_shapes=[dma((3, 4))],
+        scratch_shapes=[dma((3, 7))],
         compiler_params=pltpu.CompilerParams(vmem_limit_bytes=4 * 1024 * 1024),
         name="store_results",
     )(*(pltpu.with_memory_space_constraint(value, pltpu.VMEM) for value in (input_grad, momentum_out, update)))

time: 51.7 us -> 51.2 us (level)
    pallas_call x1, Pallas kernels: 48.4 us -> 47.8 us  [body(): pl.pallas_call(kernel, out_shape=outs, in_specs=[hbm] * 7, out_specs=(vme...]
where the time goes in v4:
time: 51.2 us; the launch traced here: 51.1 us
  Pallas kernels  50.5 us (99%)
  between operations  0.64 us (1%)
    pallas_call x1, Pallas kernels, body(): pl.pallas_call(kernel, out_shape=outs, in_specs=[hbm] * 7, out_specs=(vme...  47.8 us
    pallas_call x1, Pallas kernels, body(): pl.pallas_call(store, out_shape=outs, in_specs=[pl.BlockSpec(memory_space...  2.66 us

profile of v4, /device:TPU:2, one launch (start us, length us, event | category | flops | bytes accessed | tf_op | source)
XLA Modules:
  0.0 51.1 jit_solution(11822258845143650992)
XLA Ops:
  0.6 47.8 %demo_step.1 = (bf16[1024,128]{1,0:T(8,128)(2,1)S(1)}, f32[448,2048]{1,0:T(8,128)S(1)}, bf16[448,2048]{1,0:T(8,128)(2,1)S(1)}) custom-call(bf16[2,2,256,128]{3,2,1,0:T(8,128)(2,1)} %bitcast.14, bf16[448,1024]{1,0:T(8,128)(2,1)} %bitcast.13, bf16[448,2048]{1,0:T(8,128)(2,1)} %bitcast.12, f32[448,2048]{1,0:T(8,128)} %bitcast.11, s32[7,16,32]{2,1,0:T(8,128)} %bitcast.15, ...), custom_call_target="tpu_custom_call" | custom-call | tf_op jit(solution)/shard_map/demo_step/pallas_call | solution.py:436
  48.5 2.7 %store_results.1 = (bf16[1024,128]{1,0:T(8,128)(2,1)}, f32[448,2048]{1,0:T(8,128)}, bf16[448,2048]{1,0:T(8,128)(2,1)}) custom-call(bf16[1024,128]{1,0:T(8,128)(2,1)S(1)} %get-tuple-element.9.refs_0_, f32[448,2048]{1,0:T(8,128)S(1)} %get-tuple-element.10.refs_1_, bf16[448,2048]{1,0:T(8,128)(2,1)S(1)} %get-tuple-element.11.refs_2_), custom_call_target="tpu_custom_call" | custom-call | tf_op jit(solution)/shard_map/store_results/pallas_call | solution.py:490

commit v5 on v4

--- a/solution.py
+++ b/solution.py
@@ -271,23 +271,28 @@
         u = x_ * 2 + z_
         cols = pl.ds(pl.multiple_of(u * 256, 256), 256)
         both = jnp.concatenate([acts[2 * u].reshape(1024, 128), acts[2 * u + 1].reshape(1024, 128)], axis=1)
-        gtmp[...] = jnp.dot(got[...], both, preferred_element_type=F32)
+        gtmp[dx] = jnp.dot(got[...], both, preferred_element_type=F32)
 
         for k in range(7):
             rows = pl.ds(k * TILE, TILE)
-            kept = decay_rate * mom[rows, cols] + gtmp[rows, :]
-            gtmp[rows, :] = kept
+            kept = decay_rate * mom[rows, cols] + gtmp[dx, rows, :]
+            gtmp[dx, rows, :] = kept
             scaled = kept * basis[k : k + 1, cols]
             high = scaled.astype(BF16)
             low = (scaled - high.astype(F32)).astype(BF16)
-            ycat[rows, :] = jnp.concatenate([high, low], axis=1)
-
-        ptmp[...] = jnp.dot(ycat[...], segments[...], preferred_element_type=F32)
-        lines = lax.dot_general(chooser, ycat[...], (((1,), (1,)), ((), ())), preferred_element_type=F32)
+            ycat[dx, rows, :] = jnp.concatenate([high, low], axis=1)
+
+        lines = lax.dot_general(chooser, ycat[dx], (((1,), (1,)), ((), ())), preferred_element_type=F32)
         p_own[zi, dx // 2, pl.ds(dx % 2 * 4, 4), :] = lines[:4]
+        if zi == 0:
+            settle(dx, x_, z_)
+
+    def settle(dx, x_, z_):
+        cols = pl.ds(pl.multiple_of((x_ * 2 + z_) * 256, 256), 256)
+        ptmp[...] = jnp.dot(ycat[dx], segments[...], preferred_element_type=F32)
         for k in range(7):
             rows = pl.ds(k * TILE, TILE)
-            mom[rows, cols] = gtmp[rows, :] - ptmp[rows, :] * basis[k : k + 1, cols]
+            mom[rows, cols] = gtmp[dx, rows, :] - ptmp[rows, :] * basis[k : k + 1, cols]
 
     sb = lambda x_, z_: block(x_, z_, 1 - c)
     sh = lambda x_, z_, h: half(x_, z_, 1 - c, h)
@@ -394,7 +399,11 @@
         push(sz.at[k], rz.at[k], zs_send.at[k], zs_recv.at[k], zdev)
     rs_second(1)
 
+    settle(0, x, other)
+    settle(1, xl, other)
     p_y(3)
+    settle(2, xr, other)
+    settle(3, xo, other)
     finish(0)
     finish(1)
     finish(2)
@@ -448,9 +457,9 @@
             pltpu.VMEM((2, 3, 2, 528, 128), jnp.int16),
             pltpu.VMEM((2, 528, 128), jnp.int16),
             pltpu.VMEM((2, 528, 128), jnp.int16),
+            pltpu.VMEM((4, 448, 256), F32),
             pltpu.VMEM((448, 256), F32),
-            pltpu.VMEM((448, 256), F32),
-            pltpu.VMEM((448, 512), BF16),
+            pltpu.VMEM((4, 448, 512), BF16),
             pltpu.VMEM((7, 2048), F32),
             pltpu.VMEM((512, 256), BF16),
             pltpu.VMEM((8, 7, 128, 256), BF16),

time: 51.2 us -> 51.5 us (level)
  no operation moved by 1% of the time
where the time goes in v5:
time: 51.5 us; the launch traced here: 51.4 us
  Pallas kernels  50.7 us (98%)
  between operations  0.64 us (1%)
    pallas_call x1, Pallas kernels, body(): pl.pallas_call(kernel, out_shape=outs, in_specs=[hbm] * 7, out_specs=(vme...  48.1 us
    pallas_call x1, Pallas kernels, body(): pl.pallas_call(store, out_shape=outs, in_specs=[pl.BlockSpec(memory_space...  2.66 us

profile of v5, /device:TPU:2, one launch (start us, length us, event | category | flops | bytes accessed | tf_op | source)
XLA Modules:
  0.0 51.4 jit_solution(6667883090390025910)
XLA Ops:
  0.6 48.1 %demo_step.1 = (bf16[1024,128]{1,0:T(8,128)(2,1)S(1)}, f32[448,2048]{1,0:T(8,128)S(1)}, bf16[448,2048]{1,0:T(8,128)(2,1)S(1)}) custom-call(bf16[2,2,256,128]{3,2,1,0:T(8,128)(2,1)} %bitcast.14, bf16[448,1024]{1,0:T(8,128)(2,1)} %bitcast.13, bf16[448,2048]{1,0:T(8,128)(2,1)} %bitcast.12, f32[448,2048]{1,0:T(8,128)} %bitcast.11, s32[7,16,32]{2,1,0:T(8,128)} %bitcast.15, ...), custom_call_target="tpu_custom_call" | custom-call | tf_op jit(solution)/shard_map/demo_step/pallas_call | solution.py:445
  48.7 2.7 %store_results.1 = (bf16[1024,128]{1,0:T(8,128)(2,1)}, f32[448,2048]{1,0:T(8,128)}, bf16[448,2048]{1,0:T(8,128)(2,1)}) custom-call(bf16[1024,128]{1,0:T(8,128)(2,1)S(1)} %get-tuple-element.9.refs_0_, f32[448,2048]{1,0:T(8,128)S(1)} %get-tuple-element.10.refs_1_, bf16[448,2048]{1,0:T(8,128)(2,1)S(1)} %get-tuple-element.11.refs_2_), custom_call_target="tpu_custom_call" | custom-call | tf_op jit(solution)/shard_map/store_results/pallas_call | solution.py:499
